TPU v7x, 32 devices: a whole 2x2x4 slice. The times are simulated.
32 devices in a mesh: grp: 2 (over x), row: 16 (over z, y, core).
Axes of the slice: x: 2, y: 2, z: 4, core: 2. Of those that a mesh axis runs over, the one named last changes fastest.
Arguments:
- greens: bfloat16 [8192, 16384], P(('grp', 'row')), parts along dimension 0, may hold values from -0.0625 to 0.0625
- track_id: int32 [8192], P(('grp', 'row')), parts along dimension 0, may hold values from 0 to 7
- sigma_inv: float32 [16], P('grp'), parts along dimension 0, may hold values from 1 to 10
- sketch: float32 [192, 128, 128], P('grp', 'row'), parts along dimension 0, may hold values from -6 to 6
Outputs:
- range_basis: float32 [8192, 96], P(('grp', 'row')), parts along dimension 0
- coefficients: float32 [256, 128, 96], P(('grp', 'row')), parts along dimension 0
There are 2 independent parts, one for each index of `grp`. A program takes and returns all parts, laid end to end along the dimension named above; each array names one. Nothing has to cross between parts.
All inputs are finite; a program needn't handle non-finite values.
Results may differ from a plain program's by a relative error of at most 0.011.
Values may be sent and summed in bfloat16 or wider, within the bound.
No kernel may reach another device: no remote copies, remote signals or barrier semaphores. Data moves between devices by JAX's collectives and lax.ppermute only.
A program may use at most 128 MiB of HBM per device.

v0:
```python
import jax
import jax.numpy as jnp
from jax import lax
from jax.sharding import PartitionSpec as P

SWEEPS = 4


smoothing = 0.24


def with_halo(x, sides, width):
    for axis, dim in sides:
        count, length = (lax.axis_size(axis), x.shape[dim])
        up = [(i, (i + 1) % count) for i in range(count - 1)]
        down = [(j, i) for i, j in up]
        last = lax.slice_in_dim(x, length - width, length, axis=dim)
        initial = lax.slice_in_dim(x, 0, width, axis=dim)
        before = lax.ppermute(last, axis, up)
        after = lax.ppermute(initial, axis, down)
        x = jnp.concatenate([before, x, after], axis=dim)
    return x


def smooth_padded(padded, field):
    padded = jnp.pad(padded, ((0, 0), (0, 0), (1, 1)))
    beside_all = (
        padded[:, 2:, 1:-1] + padded[:, :-2, 1:-1] + padded[:, 1:-1, 2:] + padded[:, 1:-1, :-2]
    )
    return field + smoothing * (beside_all - 4.0 * field)


def orthonormalize(sketched, total_rows):
    local_gram = jnp.dot(sketched.T, sketched, precision=lax.Precision.HIGHEST)
    gram_matrix = lax.psum(local_gram, "row") / total_rows
    factor = jnp.linalg.cholesky(gram_matrix)
    return lax.linalg.triangular_solve(
        factor, sketched, left_side=False, lower=True, transpose_a=True
    )


def local(greens, track_id, sigma_inv, sketch):
    local_rows = greens.shape[0]
    columns_count = sketch.shape[0]
    total_rows = local_rows * lax.axis_size("row")
    row_scale = 1.0 / jnp.sqrt(jnp.float32(total_rows))
    groups = jnp.arange(sigma_inv.shape[0], dtype=jnp.int32)
    onehot = (track_id[:, None] == groups[None, :]).astype(jnp.float32)
    weights = jnp.dot(onehot, sigma_inv, precision=lax.Precision.HIGHEST)
    field = sketch
    for sweep_index in range(SWEEPS):
        padded = with_halo(field, (("row", 1),), 1)
        field = smooth_padded(padded, field)
    omega = field.astype(jnp.bfloat16)
    portion = lax.all_gather(omega, "row", axis=1, tiled=True)
    strike = portion.shape[2]
    width = portion.shape[1] * strike
    columns = greens
    flattened = portion.reshape(portion.shape[0], width)
    first = lax.dot_general(
        columns, flattened, (((1,), (1,)), ((), ())), preferred_element_type=jnp.float32
    )
    basis_one = orthonormalize(first * weights[:, None], total_rows)
    weighted_one = (basis_one * weights[:, None]).astype(jnp.bfloat16)
    columns = greens
    back_local = lax.psum_scatter(
        lax.dot_general(
            columns, weighted_one, (((0,), (0,)), ((), ())), preferred_element_type=jnp.float32
        ),
        "row",
        scatter_dimension=0,
        tiled=True,
    )
    back_local = (back_local * row_scale).astype(jnp.bfloat16)
    columns = greens
    second = jnp.dot(
        columns,
        lax.all_gather(back_local, "row", axis=0, tiled=True),
        preferred_element_type=jnp.float32,
    )
    range_basis = orthonormalize(second * weights[:, None], total_rows)
    weighted_two = (range_basis * weights[:, None]).astype(jnp.bfloat16)
    columns = greens
    projected = lax.psum_scatter(
        lax.dot_general(
            columns, weighted_two, (((0,), (0,)), ((), ())), preferred_element_type=jnp.float32
        ),
        "row",
        scatter_dimension=0,
        tiled=True,
    )
    coefficients = (projected * row_scale).reshape(sketch.shape[1], sketch.shape[2], columns_count)
    return (range_basis, coefficients)


def solution(mesh):
    in_specs = (P(("grp", "row"), None), P(("grp", "row")), P("grp"), P("grp", "row", None))
    out_specs = (P(("grp", "row"), None), P(("grp", "row"), None, None))
    return jax.shard_map(local, mesh=mesh, in_specs=in_specs, out_specs=out_specs, check_vma=False)
```

profile of v0, /device:TPU:0, one launch (start us, length us, event | category | flops | bytes accessed | tf_op | source)
XLA Modules:
  0.0 502.3 jit_solution(15993353237637454936)
XLA Ops:
  8.5 2.4 collective-permute-start.1
  12.2 3.9 collective-permute-done
  16.1 1.9 select_maximum_fusion.6
  18.4 4.7 collective-permute-start.3
  24.4 1.8 collective-permute-done.2
  27.5 5.0 collective-permute-start.5
  33.8 1.8 collective-permute-done.4
  36.9 5.1 %collective-permute-start.7 = (f32[96,1,128]{2,1,0:T(1,128)S(1)}, f32[96,1,128]{2,1,0:T(1,128)S(1)}, u32[]{:S(2)}, u32[]{:S(2)}) collective-permute-start(f32[96,1,128]{2,1,0:T(1,128)S(1)} %get-tuple-element.6), channel_id=1, source_target_pairs={{0,1},{1,2},{2,3},{3,4},{4,5},{5,6},{6,7},{7,8},{8,9},{9,10},{10,1... | collective-permute-start | bytes 147464 | tf_op jit(solution)/shard_map/ppermute | solution.py:19
  43.3 1.8 collective-permute-done.6
  47.3 50.3 %all-gather.3.cloned.1.call-done = bf16[96,128,128]{2,1,0:T(8,128)(2,1)} async-done(((bf16[96,8,128]{2,1,0:T(8,128)(2,1)}), bf16[96,128,128]{2,1,0:T(8,128)(2,1)}) %all-gather.3.cloned.1.call-update) | async-done | bytes 3145744 | tf_op jit(solution)/shard_map/all_gather | solution.py:55
  97.6 7.7 %fusion.5 = f32[96,256]{1,0:T(8,128)S(1)} fusion(bf16[256,16384]{1,0:T(8,128)(2,1)} %param.7, bf16[12,8,128,128]{3,2,1,0:T(8,128)(2,1)} %bitcast.61, f32[256]{0:T(256)S(1)} %bitcast.62), kind=kOutput, calls=%fused_computation.20 | convolution fusion | flops 805330944 | bytes 11633664 | tf_op jit(solution)/shard_map/dot_general | solution.py:60
  105.6 58.9 %psum.14 = f32[96,96]{0,1:T(8,128)S(1)} all-reduce(f32[96,96]{0,1:T(8,128)S(1)} %fusion.44), channel_id=1, replica_groups=mesh['grp'=2,'row'=16] {'row'}, use_global_device_ids=true, to_apply=%region_0.1 | all-reduce | flops 9216 | bytes 73728 | tf_op jit(solution)/shard_map/psum | solution.py:35
  164.6 8.8 %cholesky.44 = f32[96,96]{1,0:T(8,128)S(1)} custom-call(f32[96,96]{1,0:T(8,128)S(1)} %fusion.35), custom_call_target="Cholesky" | custom-call | tf_op jit(solution)/shard_map/jit(cholesky)/cholesky | solution.py:36
  174.7 7.4 %custom-call.6 = f32[1,96,96]{1,2,0:T(8,128)S(1)} custom-call(f32[1,96,96]{2,1,0:T(8,128)S(1)} %fusion.30), custom_call_target="InvertDiagBlocksLowerTriangular" | custom-call | tf_op jit(solution)/shard_map/triangular_solve/custom-call.0 | solution.py:37
  182.4 7.5 %convolution_bitcast_fusion.1 = f32[16384,96]{0,1:T(8,128)} fusion(bf16[256,96]{0,1:T(8,128)(2,1)S(1)} %fusion.8, bf16[256,16384]{1,0:T(8,128)(2,1)} %param.7), kind=kOutput, calls=%fused_computation.1 | convolution fusion | flops 805306368 | bytes 14729216 | tf_op jit(solution)/shard_map/dot_general | solution.py:67
  190.0 82.4 %reduce-scatter.3.cloned.1.call-done = f32[1024,96]{0,1:T(8,128)} async-done(((f32[16384,96]{0,1:T(8,128)}), f32[1024,96]{0,1:T(8,128)}) %reduce-scatter.3.cloned.1.call-update) | async-done | bytes 393232 | tf_op jit(solution)/shard_map/reduce_scatter | solution.py:66
  274.1 45.6 %all-gather.5.cloned.1.call-done = bf16[16384,96]{0,1:T(8,128)(2,1)} async-done(((bf16[1024,96]{0,1:T(8,128)(2,1)}), bf16[16384,96]{0,1:T(8,128)(2,1)}) %all-gather.5.cloned.1.call-update) | async-done | bytes 3145744 | tf_op jit(solution)/shard_map/all_gather | solution.py:78
  319.7 7.1 %convolution_multiply_fusion = f32[96,256]{1,0:T(8,128)S(1)} fusion(bf16[16384,96]{0,1:T(8,128)(2,1)} %all-gather.5.cloned.1.call-done, bf16[256,16384]{1,0:T(8,128)(2,1)} %param.7, f32[256]{0:T(256)S(1)} %bitcast.64), kind=kOutput, calls=%fused_computation.17 | convolution fusion | flops 805330944 | bytes 11633664 | tf_op jit(solution)/shard_map/dot_general | solution.py:76
  327.0 59.1 %psum.15 = f32[96,96]{0,1:T(8,128)S(1)} all-reduce(f32[96,96]{0,1:T(8,128)S(1)} %fusion.45), channel_id=1, replica_groups=mesh['grp'=2,'row'=16] {'row'}, use_global_device_ids=true, to_apply=%region_4.7 | all-reduce | flops 9216 | bytes 73728 | tf_op jit(solution)/shard_map/psum | solution.py:35
  386.3 8.8 %cholesky.55 = f32[96,96]{1,0:T(8,128)S(1)} custom-call(f32[96,96]{1,0:T(8,128)S(1)} %fusion.33), custom_call_target="Cholesky" | custom-call | tf_op jit(solution)/shard_map/jit(cholesky)/cholesky | solution.py:36
  396.4 7.4 %custom-call.7 = f32[1,96,96]{1,2,0:T(8,128)S(1)} custom-call(f32[1,96,96]{2,1,0:T(8,128)S(1)} %fusion.31), custom_call_target="InvertDiagBlocksLowerTriangular" | custom-call | tf_op jit(solution)/shard_map/triangular_solve/custom-call.0 | solution.py:37
  404.0 7.5 %convolution_bitcast_fusion = f32[16384,96]{0,1:T(8,128)} fusion(bf16[256,16384]{1,0:T(8,128)(2,1)} %param.7, f32[256,96]{0,1:T(8,128)S(1)} %convolution_bitcast_fusion.2, f32[256]{0:T(256)S(1)} %bitcast.65), kind=kOutput, calls=%fused_computation | convolution fusion | flops 805355520 | bytes 14779392 | tf_op jit(solution)/shard_map/dot_general | solution.py:85
  411.6 82.4 %reduce-scatter.5.cloned.1.call-done = f32[1024,96]{0,1:T(8,128)} async-done(((f32[16384,96]{0,1:T(8,128)}), f32[1024,96]{0,1:T(8,128)}) %reduce-scatter.5.cloned.1.call-update) | async-done | bytes 393232 | tf_op jit(solution)/shard_map/reduce_scatter | solution.py:84
  494.0 1.8 copy_bitcast_fusion
  (53 shorter events, 17.3 us)
Async XLA Ops:
  7.2 40.0 %copy-start = (f32[8]{0:T(128)S(1)}, f32[8]{0:T(128)}, u32[]{:S(2)}) copy-start(f32[8]{0:T(128)} %param.9) | copy-start | bytes 100
  7.2 10.8 %copy-start.1 = (f32[96,8,128]{2,1,0:T(8,128)S(1)}, f32[96,8,128]{2,1,0:T(8,128)}, u32[]{:S(2)}) copy-start(f32[96,8,128]{2,1,0:T(8,128)} %param.10) | copy-start | bytes 1179652
  7.2 90.5 %all-gather.3.cloned.1.call-start = ((), (), s32[]{:S(2)}) async-start(), calls=%async_computation.2 | async-start | bytes 3342336 | tf_op jit(solution)/shard_map/all_gather | solution.py:55
  8.5 3.7 collective-permute-start.1
  10.9 5.2 %collective-permute-start = (f32[96,1,128]{2,1,0:T(1,128)S(1)}, f32[96,1,128]{2,1,0:T(1,128)S(1)}, u32[]{:S(2)}, u32[]{:S(2)}) collective-permute-start(f32[96,1,128]{2,1,0:T(1,128)S(1)} %get-tuple-element.13), channel_id=1, source_target_pairs={{1,0},{2,1},{3,2},{4,3},{5,4},{6,5},{7,6},{8,7},{9,8},{10,9},{11,1... | collective-permute-start | bytes 147464 | tf_op jit(solution)/shard_map/ppermute | solution.py:20
  18.4 6.0 %collective-permute-start.3 = (f32[96,1,128]{2,1,0:T(1,128)S(1)}, f32[96,1,128]{2,1,0:T(1,128)S(1)}, u32[]{:S(2)}, u32[]{:S(2)}) collective-permute-start(f32[96,1,128]{2,1,0:T(1,128)S(1)} %get-tuple-element.10), channel_id=1, source_target_pairs={{0,1},{1,2},{2,3},{3,4},{4,5},{5,6},{6,7},{7,8},{8,9},{9,10},{10,1... | collective-permute-start | bytes 147464 | tf_op jit(solution)/shard_map/ppermute | solution.py:19
  23.1 3.1 collective-permute-start.2
  27.5 6.3 %collective-permute-start.5 = (f32[96,1,128]{2,1,0:T(1,128)S(1)}, f32[96,1,128]{2,1,0:T(1,128)S(1)}, u32[]{:S(2)}, u32[]{:S(2)}) collective-permute-start(f32[96,1,128]{2,1,0:T(1,128)S(1)} %get-tuple-element.8), channel_id=1, source_target_pairs={{0,1},{1,2},{2,3},{3,4},{4,5},{5,6},{6,7},{7,8},{8,9},{9,10},{10,1... | collective-permute-start | bytes 147464 | tf_op jit(solution)/shard_map/ppermute | solution.py:19
  32.5 3.1 collective-permute-start.4
  36.9 6.4 %collective-permute-start.7 = (f32[96,1,128]{2,1,0:T(1,128)S(1)}, f32[96,1,128]{2,1,0:T(1,128)S(1)}, u32[]{:S(2)}, u32[]{:S(2)}) collective-permute-start(f32[96,1,128]{2,1,0:T(1,128)S(1)} %get-tuple-element.6), channel_id=1, source_target_pairs={{0,1},{1,2},{2,3},{3,4},{4,5},{5,6},{6,7},{7,8},{8,9},{9,10},{10,1... | collective-permute-start | bytes 147464 | tf_op jit(solution)/shard_map/ppermute | solution.py:19
  42.0 5.1 %copy-start.3 = (s32[256]{0:T(256)S(1)}, s32[256]{0:T(256)}, u32[]{:S(2)}) copy-start(s32[256]{0:T(256)} %param.8) | copy-start | bytes 3076
  42.0 3.1 collective-permute-start.6
  47.1 225.3 %reduce-scatter.3.cloned.1.call-start = ((), (), s32[]{:S(2)}) async-start(), calls=%async_computation.3 | async-start | bytes 6684672 | tf_op jit(solution)/shard_map/reduce_scatter | solution.py:66
  189.9 129.8 %all-gather.5.cloned.1.call-start = ((), (), s32[]{:S(2)}) async-start(), calls=%async_computation.4 | async-start | bytes 3342336 | tf_op jit(solution)/shard_map/all_gather | solution.py:78
  274.1 219.9 %reduce-scatter.5.cloned.1.call-start = ((), (), s32[]{:S(2)}) async-start(), calls=%async_computation.5 | async-start | bytes 6684672 | tf_op jit(solution)/shard_map/reduce_scatter | solution.py:84
  404.0 7.5 %copy-start.2 = (f32[256,96]{0,1:T(8,128)}, f32[256,96]{0,1:T(8,128)S(1)}, u32[]{:S(2)}) copy-start(f32[256,96]{0,1:T(8,128)S(1)} %convolution_bitcast_fusion.2) | copy-start | bytes 294916
Sparse Core Ops, SparseCore 0:
  47.2 50.3 all-gather.2
  190.0 82.2 reduce-scatter.2
  275.1 44.5 all-gather.4
  411.7 82.2 reduce-scatter.4
where the time goes:
time: 503 us; the launch traced here: 502 us
  waiting for transfers between devices  270 us (54%)
  blocking collectives  118 us (23%)
  other arithmetic  44.9 us (9%)
  matrix products  31.1 us (6%)
  starting transfers between devices  22.5 us (4%)
  between operations  14.1 us (3%)
    psum x2, blocking collectives, orthonormalize(): gram_matrix = lax.psum(local_gram, 'row') / total_rows  118 us
    reduce_scatter x1, waiting for transfers between devices, local(): lax.psum_scatter(lax.dot_general(columns, weighted_one, (((0,), (0,)), ((...  82.4 us
    reduce_scatter x1, waiting for transfers between devices, local(): lax.psum_scatter(lax.dot_general(columns, weighted_two, (((0,), (0,)), ((...  82.4 us
    all_gather x1, waiting for transfers between devices, local(): portion = lax.all_gather(omega, 'row', axis=1, tiled=True)  50.3 us
    all_gather x1, waiting for transfers between devices, local(): lax.all_gather(back_local, 'row', axis=0, tiled=True)  45.6 us
    another operation x6, other arithmetic, orthonormalize(): factor = jnp.linalg.cholesky(gram_matrix)  18.9 us
    ppermute x4, starting transfers between devices, with_halo(): before = lax.ppermute(last, axis, up)  17.2 us
    another operation x4, other arithmetic, orthonormalize(): lax.linalg.triangular_solve(factor, sketched, left_side=False, lower=True...  16 us
  transfers between devices with their start and end apart: 12, of which 8 were waited for; matrix products, arithmetic and copies ran while one was open for 0% of the time, Pallas kernels for 0%

commit v1 on v0

v1 whole, which is shorter than its diff:
```python
import functools

import jax
import jax.numpy as jnp
from jax import lax
from jax.experimental import pallas as pl
from jax.experimental.pallas import tpu as pltpu
from jax.sharding import PartitionSpec as P


SWEEPS = 4
smoothing = 0.24
HIGH = lax.Precision.HIGHEST
f32, bf16 = jnp.float32, jnp.bfloat16
NT = (((1,), (1,)), ((), ()))
VM = pltpu.VMEM


def swap(x, k):
    n = lax.axis_size("row")
    return lax.ppermute(x, "row", [(i, i ^ k) for i in range(n)])


def halo_rows(x, width):
    n, length = lax.axis_size("row"), x.shape[1]
    hops = -(-width // length)
    before, after = [], []
    for hop in range(1, hops + 1):
        take = min(length, width - (hop - 1) * length)
        up = [(i, i + hop) for i in range(n - hop)]
        down = [(j, i) for i, j in up]
        before.insert(0, lax.ppermute(x[:, length - take:], "row", up))
        after.append(lax.ppermute(x[:, :take], "row", down))
    return jnp.concatenate(before, axis=1), jnp.concatenate(after, axis=1)


def smooth_kernel(edge_ref, before_ref, own_ref, after_ref, out_ref):
    columns, length, strike = own_ref.shape
    width = before_ref.shape[1]
    top, bottom = edge_ref[0], edge_ref[1]
    shape = (8, strike)
    lane = lax.broadcasted_iota(jnp.int32, shape, 1)
    from_left = jnp.where(lane == 0, 0.0, smoothing)
    from_right = jnp.where(lane == strike - 1, 0.0, smoothing)
    inside = [jnp.where(jnp.full(shape, i, jnp.int32) >= width - top, 1.0, 0.0) for i in range(width)]
    inside += [None] * length
    inside += [jnp.where(jnp.full(shape, i, jnp.int32) < bottom, 1.0, 0.0) for i in range(width)]

    def group(g, _):
        at = pl.ds(pl.multiple_of(g * 8, 8), 8)
        rows = [before_ref[at, i, :] for i in range(width)]
        rows += [own_ref[at, i, :] for i in range(length)]
        rows += [after_ref[at, i, :] for i in range(width)]
        for sweep in range(width):
            new = list(rows)
            for i in range(sweep + 1, len(rows) - sweep - 1):
                v = rows[i]
                u = v * (1.0 - 4.0 * smoothing) + smoothing * (rows[i + 1] + rows[i - 1])
                u = u + from_left * pltpu.roll(v, 1, 1) + from_right * pltpu.roll(v, strike - 1, 1)
                new[i] = u if inside[i] is None else u * inside[i]
            rows = new
        for i in range(length):
            out_ref[at, i * strike:(i + 1) * strike] = rows[width + i].astype(bf16)
        return 0

    lax.fori_loop(0, columns // 8, group, 0, unroll=2)


def smooth(sketch):
    columns, length, strike = sketch.shape
    n, me = lax.axis_size("row"), lax.axis_index("row")
    before, after = halo_rows(sketch, SWEEPS)
    top = jnp.minimum(me * length, SWEEPS)
    bottom = jnp.minimum((n - 1 - me) * length, SWEEPS)
    return pl.pallas_call(
        smooth_kernel,
        out_shape=jax.ShapeDtypeStruct((columns, length * strike), bf16),
        in_specs=[pl.BlockSpec(memory_space=pltpu.SMEM)] + [pl.BlockSpec(memory_space=VM)] * 3,
        out_specs=pl.BlockSpec(memory_space=VM),
        compiler_params=pltpu.CompilerParams(vmem_limit_bytes=16 << 20),
        name="smooth",
    )(jnp.stack([top, bottom]).astype(jnp.int32), before, sketch, after)


def inverse_kernel(total, gram_ref, out_ref, *, step=8):
    size = gram_ref.shape[0]
    groups = size // 8
    shape = (8, size)
    lane = lax.broadcasted_iota(jnp.int32, shape, 1)
    sub = lax.broadcasted_iota(jnp.int32, shape, 0)
    full = lambda v: jnp.broadcast_to(v, shape)
    rows = [gram_ref[8 * g:8 * g + 8, :] * (1.0 / total) for g in range(groups)]
    scale = [None] * groups
    for j in range(0, size, step):
        g, s = j // 8, j % 8
        below = range(groups - g)
        cols = [[full(rows[g + h][:, j + q:j + q + 1]) for h in below] for q in range(step)]
        block = (lane >= j) & (lane < j + step)
        unit = lambda q: jnp.where(lane == j + q, 1.0, 0.0)
        pivots = [jnp.where(block, unit(q), full(rows[g][s + q:s + q + 1, :])) for q in range(step)]
        p = [[full(cols[t][0][s + q:s + q + 1, :]) for t in range(q + 1)] for q in range(step)]
        rest = [jnp.where(block, 0.0, rows[g + h]) for h in below]
        for q in range(step):
            inv = 1.0 / p[q][q]
            root = lax.rsqrt(p[q][q])
            scale[g] = root if scale[g] is None else jnp.where(sub >= s + q, root, scale[g])
            for r in range(q + 1, step):
                m = p[r][q] * inv
                for t in range(q + 1, r + 1):
                    p[r][t] = p[r][t] - m * p[t][q]
                pivots[r] = pivots[r] - m * pivots[q]
            for h in below:
                f = cols[q][h] * inv
                for t in range(q + 1, step):
                    cols[t][h] = cols[t][h] - f * p[t][q]
                rest[h] = rest[h] - f * pivots[q]
        for h in below:
            rows[g + h] = rest[h] if h else jnp.where(sub < s, rows[g], rest[0])
        for q in range(step):
            rows[g] = jnp.where(sub == s + q, pivots[q], rows[g])
    for g in range(groups):
        index = 8 * g + sub
        lower = jnp.where(lane < index, rows[g], jnp.where(lane == index, 1.0, 0.0))
        out_ref[8 * g:8 * g + 8, :] = lower * scale[g]


def small_call(kernel, outs, args, smem=0, scratch=()):
    spaces = [pltpu.SMEM] * smem + [VM] * (len(args) - smem)
    many = isinstance(outs, list)
    return pl.pallas_call(
        kernel,
        out_shape=outs,
        in_specs=[pl.BlockSpec(memory_space=m) for m in spaces],
        out_specs=[pl.BlockSpec(memory_space=VM)] * len(outs) if many else pl.BlockSpec(memory_space=VM),
        scratch_shapes=list(scratch),
        compiler_params=pltpu.CompilerParams(vmem_limit_bytes=16 << 20),
    )(*args)


def inverse_factor(gram, total):
    return small_call(functools.partial(inverse_kernel, float(total)), jax.ShapeDtypeStruct(gram.shape, f32),
                      [gram])


def copy_blocks(pairs, sem):
    copies = [pltpu.make_async_copy(a, b, sem.at[i]) for i, (a, b) in enumerate(pairs)]
    for c in copies:
        c.start()
    for c in copies:
        c.wait()


def pick_kernel(core_ref, in_ref, out_ref, sem):
    chips, _, block = out_ref.shape
    at = lambda m: pl.ds(pl.multiple_of((2 * m + core_ref[0]) * block, block), block)
    copy_blocks([(in_ref.at[:, at(m)], out_ref.at[m]) for m in range(chips)], sem)


def pick(greens, core, chips, block, out):
    return pl.pallas_call(
        pick_kernel,
        out_shape=out((chips, greens.shape[0], block), greens.dtype),
        in_specs=[pl.BlockSpec(memory_space=pltpu.SMEM), pl.BlockSpec(memory_space=pltpu.HBM)],
        out_specs=pl.BlockSpec(memory_space=VM),
        scratch_shapes=[pltpu.SemaphoreType.DMA((chips,))],
        compiler_params=pltpu.CompilerParams(vmem_limit_bytes=16 << 20),
    )(core[None], greens)


def keep_kernel(in_ref, out_ref, sem):
    copy_blocks([(in_ref.at[m], out_ref.at[m]) for m in range(out_ref.shape[0])], sem)


def keep(x):
    return pl.pallas_call(
        keep_kernel,
        out_shape=VM(x.shape, x.dtype),
        in_specs=[pl.BlockSpec(memory_space=pltpu.HBM)],
        out_specs=pl.BlockSpec(memory_space=VM),
        scratch_shapes=[pltpu.SemaphoreType.DMA((x.shape[0],))],
        compiler_params=pltpu.CompilerParams(vmem_limit_bytes=16 << 20),
        name="keep_theirs",
    )(x)


def forward_kernel(slots, seeded, last, chip_ref, mine_ref, theirs_ref, *refs):
    parts, rest = refs[:len(slots)], refs[len(slots):]
    rows = mine_ref.shape[1]
    a = rest[0][:, :rows] if seeded else 0.0
    b = rest[0][:, rows:] if seeded else 0.0
    for slot, part_ref in zip(slots, parts):
        m = chip_ref[0] ^ slot
        part = part_ref[...]
        a += lax.dot_general(part, mine_ref[m], NT, preferred_element_type=f32)
        b += lax.dot_general(part, theirs_ref[m], NT, preferred_element_type=f32)
    out_ref = rest[1 if seeded else 0]
    out_ref[:, :rows] = a
    out_ref[:, rows:] = b
    if last:
        rest[-1][:, :rows] = b
        rest[-1][:, rows:] = a


def forward_call(chip, mine, theirs, stage, seed, last):
    slots, parts = [s for s, _ in stage], [p for _, p in stage]
    seeds = [] if seed is None else [seed]
    shape = jax.ShapeDtypeStruct((parts[0].shape[0], 2 * mine.shape[1]), f32)
    return small_call(functools.partial(forward_kernel, slots, seed is not None, last),
                      [shape, shape] if last else shape, [chip[None], mine, theirs] + parts + seeds,
                      smem=1)


def finish_kernel(whitened, total_ref, other_ref, weights_ref, *refs):
    y = (total_ref[...] + other_ref[...]) * weights_ref[...]
    if whitened:
        y = jnp.dot(refs[0][...], y, precision=HIGH, preferred_element_type=f32)
    y_ref, weighted_ref, gram_ref = refs[-3:]
    y_ref[...] = y
    weighted_ref[...] = (y * weights_ref[...]).astype(bf16)
    gram_ref[...] = lax.dot_general(y, y, NT, precision=HIGH, preferred_element_type=f32)


def finish(total, other, weights, white):
    columns = total.shape[0]
    outs = [jax.ShapeDtypeStruct(total.shape, f32), jax.ShapeDtypeStruct(total.shape, bf16),
            jax.ShapeDtypeStruct((columns, columns), f32)]
    return small_call(functools.partial(finish_kernel, white is not None), outs,
                      [total, other, weights] + ([] if white is None else [white]))


def backward_kernel(slots, chip_ref, mine_ref, theirs_ref, y_ref, *outs):
    rows = mine_ref.shape[1]
    for slot, out_ref in zip(slots, outs):
        m = chip_ref[0] ^ slot
        v = jnp.dot(y_ref[:, :rows], mine_ref[m], preferred_element_type=f32)
        v += jnp.dot(y_ref[:, rows:], theirs_ref[m], preferred_element_type=f32)
        out_ref[...] = v.astype(out_ref.dtype)


def backward_call(chip, mine, theirs, weighted, slots, dtype):
    shape = jax.ShapeDtypeStruct((weighted.shape[0], mine.shape[2]), dtype)
    return small_call(functools.partial(backward_kernel, slots), [shape] * len(slots),
                      [chip[None], mine, theirs, weighted], smem=1)


def back_kernel(scale, inv_ref, own_ref, *refs):
    total = own_ref[...]
    for r in refs[:-1]:
        total = total + r[...].astype(f32)
    refs[-1][...] = (jnp.dot(inv_ref[...], total, precision=HIGH, preferred_element_type=f32) * scale).astype(bf16)


def order(chips):
    return [0, 2, 6, 4] if chips == 8 else [2 * k for k in range(chips // 2)]


def gram_sum(x, steps):
    for k in steps:
        x = x + swap(x, k)
    return x


def local(greens, track_id, sigma_inv, sketch):
    n = lax.axis_size("row")
    chips = n // 2
    rows, params = greens.shape
    columns, length, strike = sketch.shape
    block = params // n
    total_rows = rows * n
    row_scale = 1.0 / jnp.sqrt(f32(total_rows))
    me = lax.axis_index("row")
    core, chip = me % 2, me // 2

    groups = jnp.arange(sigma_inv.shape[0], dtype=jnp.int32)
    onehot = (track_id[:, None] == groups[None, :]).astype(f32)
    weights = jnp.dot(onehot, sigma_inv, precision=HIGH)
    weights = jnp.concatenate([weights, swap(weights, 1)])

    weights = weights[None, :]
    omega = smooth(sketch)
    sent = pick(pltpu.with_memory_space_constraint(greens, pltpu.HBM), 1 - core, chips, block,
                jax.ShapeDtypeStruct)
    theirs = swap(sent, 1)
    theirs = keep(theirs)
    mine = pick(pltpu.with_memory_space_constraint(greens, pltpu.HBM), core, chips, block, VM)

    def forward(own):
        near, ks = {}, order(chips)
        for k in ks:
            near[k] = own if k == 0 else swap(own, 2 * k)
        across = {k: swap(near[k], 2) for k in ks}
        stages = [[(k, near[k]) for k in ks[:-1]] + [(k + 1, across[k]) for k in ks[:-2]],
                  [(k, near[k]) for k in ks[-1:]] + [(k + 1, across[k]) for k in ks[-2:-1]],
                  [(ks[-1] + 1, across[ks[-1]])]]
        total = None
        for i, stage in enumerate(stages):
            total = forward_call(chip, mine, theirs, stage, total, i == len(stages) - 1)
        return total[0], swap(total[1], 1)

    def backward(weighted):
        ks = order(chips)[::-1]

        def call(slots, dtype):
            return backward_call(chip, mine, theirs, weighted, slots, dtype)

        sent = call([ks[0] + 1], bf16) + call([k + 1 for k in ks[1:]], bf16)
        kept = call(ks, f32)
        sums = [a + swap(v, 2).astype(f32) for a, v in zip(kept, sent)]
        far = [swap(v.astype(bf16), 2 * k) for v, k in zip(sums, ks) if k]
        return [sums[-1]] + far

    slower = [1 << i for i in range(2, n.bit_length() - 1)]
    gram0 = gram_sum(lax.dot_general(omega, omega, NT, preferred_element_type=f32), [1, 2] + slower)
    white = inverse_factor(gram0, params)
    _, weighted, gram = finish(*forward(omega), weights, white)
    pieces = backward(weighted)
    inv_one = inverse_factor(gram_sum(gram, slower + [2]), total_rows)
    back = small_call(functools.partial(back_kernel, float(total_rows) ** -0.5),
                      jax.ShapeDtypeStruct((columns, block), bf16), [inv_one] + pieces)
    second, weighted, gram = finish(*forward(back), weights, None)
    pieces = backward(weighted)
    inv_two = inverse_factor(gram_sum(gram, slower + [2]), total_rows)
    projected = sum([v.astype(f32) for v in pieces[1:]], pieces[0])
    range_basis = lax.dot_general(second[:, :rows], inv_two, (((0,), (1,)), ((), ())), precision=HIGH)
    coefficients = lax.dot_general(projected, inv_two, (((0,), (1,)), ((), ())), precision=HIGH) * row_scale
    return (range_basis, coefficients.reshape(length, strike, columns))


def solution(mesh):
    in_specs = (P(("grp", "row"), None), P(("grp", "row")), P("grp"), P("grp", "row", None))
    out_specs = (P(("grp", "row"), None), P(("grp", "row"), None, None))

    return jax.shard_map(local, mesh=mesh, in_specs=in_specs, out_specs=out_specs, check_vma=False)
```

time: 503 us -> 164 us (0.33)
  waiting for transfers between devices: 270 us -> 73.2 us
  blocking collectives: 118 us -> 0 us
  other arithmetic: 44.9 us -> 0.47 us
  Pallas kernels: 0 us -> 33.2 us
  matrix products: 31.1 us -> 1.88 us
  starting transfers between devices: 22.5 us -> 50.7 us
  between operations: 14.1 us -> 1.04 us
    reduce_scatter x2 -> x0, waiting for transfers between devices: 165 us -> none  [the longest x1 82.4 us: local(): lax.psum_scatter(lax.dot_general(columns, weighted_one, (((0,), (0,)), ((...]
    psum x2 -> x0, blocking collectives: 118 us -> none  [orthonormalize(): gram_matrix = lax.psum(local_gram, 'row') / total_rows]
    all_gather x2 -> x0, waiting for transfers between devices: 95.9 us -> none  [the longest x1 50.3 us: local(): portion = lax.all_gather(omega, 'row', axis=1, tiled=True)]
    ppermute x8 -> x44, waiting for transfers between devices: 9.39 us -> 73.2 us  [the longest x42 69.2 us: swap(): return lax.ppermute(x, 'row', [(i, i ^ k) for i in range(n)])]
    another operation x10 -> x1, other arithmetic: 34.9 us -> 0.08 us  [smooth(): jnp.stack([top, bottom]).astype(jnp.int32)]
    pallas_call x0 -> x22, Pallas kernels: none -> 33.2 us  [the longest x18 20.6 us: small_call(): pl.pallas_call(kernel, out_shape=outs, in_specs=[pl.BlockSpec(memory_spac...]
    dot_general x7 -> x4, matrix products: 30.5 us -> 1.88 us  [the longest x1 0.88 us: local(): lax.dot_general(second[:, :rows], inv_two, (((0,), (1,)), ((), ())), prec...]
    ppermute x8 -> x44, starting transfers between devices: 22.4 us -> 50.7 us  [the longest x42 47.5 us: swap(): return lax.ppermute(x, 'row', [(i, i ^ k) for i in range(n)])]
  transfers between devices with their start and end apart: 12 -> 44, of which waited for: 8 -> 25; matrix products, arithmetic and copies ran while one was open for 0% -> 1% of each run, Pallas kernels for 0% -> 16%
where the time goes in v1:
time: 164 us
  waiting for transfers between devices  73.2 us (45%)
  starting transfers between devices  50.7 us (31%)
  Pallas kernels  33.2 us (20%)
  local copies, waits for them, and re-layouts  3.15 us (2%)
  matrix products  1.88 us (1%)
    ppermute x42, waiting for transfers between devices, swap(): return lax.ppermute(x, 'row', [(i, i ^ k) for i in range(n)])  69.2 us
    ppermute x42, starting transfers between devices, swap(): return lax.ppermute(x, 'row', [(i, i ^ k) for i in range(n)])  47.5 us
    pallas_call x18, Pallas kernels, small_call(): pl.pallas_call(kernel, out_shape=outs, in_specs=[pl.BlockSpec(memory_spac...  20.6 us
    pallas_call x2, Pallas kernels, pick(): pl.pallas_call(pick_kernel, out_shape=out((chips, greens.shape[0], block)...  6.5 us
    ppermute x1, waiting for transfers between devices, halo_rows(): before.insert(0, lax.ppermute(x[:, length - take:], 'row', up))  3.87 us
    pallas_call x1, Pallas kernels, smooth(): pl.pallas_call(smooth_kernel, out_shape=jax.ShapeDtypeStruct((columns, le...  3.54 us
  transfers between devices with their start and end apart: 44, of which 25 were waited for; matrix products, arithmetic and copies ran while one was open for 1% of the time, Pallas kernels for 16%

profile of v1, /device:TPU:0, one launch (start us, length us, event | category | flops | bytes accessed | tf_op | source)
XLA Modules:
  0.0 163.6 jit_solution(7449776053885769950)
XLA Ops:
  0.7 4.3 %shard_map.60 = bf16[8,256,1024]{2,1,0:T(8,128)(2,1)} custom-call(s32[1]{0:T(128)} %bitcast.2.core_ref, bf16[256,16384]{1,0:T(8,128)(2,1)} %in_ref.3), custom_call_target="tpu_custom_call" | custom-call | tf_op jit(solution)/shard_map/pallas_call | solution.py:160
  8.9 3.9 %collective-permute-done.1.before_ref = f32[96,4,128]{2,1,0:T(4,128)S(1)} collective-permute-done((f32[96,4,128]{2,1,0:T(4,128)S(1)}, f32[96,4,128]{2,1,0:T(4,128)S(1)}, u32[]{:S(2)}, u32[]{:S(2)}) %collective-permute-start.1) | collective-permute-done | bytes 196640 | tf_op jit(solution)/shard_map/ppermute | solution.py:32
  13.0 3.5 %smooth.1.refs_0_ = bf16[96,1024]{1,0:T(8,128)(2,1)S(1)} custom-call(s32[2]{0:T(128)S(1)} %pad_add_fusion.edge_ref, f32[96,4,128]{2,1,0:T(4,128)S(1)} %collective-permute-done.1.before_ref, f32[96,8,128]{2,1,0:T(8,128)S(1)} %copy-done.3, f32[96,4,128]{2,1,0:T(4,128)S(1)} %collective-permute-done.2.after_ref), custom_call_target="tpu_custom_call" | custom-call | tf_op jit(solution)/shard_map/smooth/pallas_call | solution.py:75
  16.5 4.9 %collective-permute-start.7 = (bf16[96,1024]{1,0:T(8,128)(2,1)S(1)}, bf16[96,1024]{1,0:T(8,128)(2,1)S(1)}, u32[]{:S(2)}, u32[]{:S(2)}) collective-permute-start(bf16[96,1024]{1,0:T(8,128)(2,1)S(1)} %smooth.1.refs_0_), channel_id=1, source_target_pairs={{0,4},{1,5},{2,6},{3,7},{4,0},{5,1},{6,2},{7,3},{8,12},{9,13},{10,... | collective-permute-start | bytes 589832 | tf_op jit(solution)/shard_map/ppermute | solution.py:21
  21.4 2.5 %collective-permute-start.5 = (bf16[96,1024]{1,0:T(8,128)(2,1)S(1)}, bf16[96,1024]{1,0:T(8,128)(2,1)S(1)}, u32[]{:S(2)}, u32[]{:S(2)}) collective-permute-start(bf16[96,1024]{1,0:T(8,128)(2,1)S(1)} %smooth.1.refs_0_), channel_id=1, source_target_pairs={{0,12},{1,13},{2,14},{3,15},{4,8},{5,9},{6,10},{7,11},{8,4},{9,5},... | collective-permute-start | bytes 589832 | tf_op jit(solution)/shard_map/ppermute | solution.py:21
  34.0 8.4 %collective-permute-done.3.refs_0_ = bf16[96,1024]{1,0:T(8,128)(2,1)S(1)} collective-permute-done((bf16[96,1024]{1,0:T(8,128)(2,1)S(1)}, bf16[96,1024]{1,0:T(8,128)(2,1)S(1)}, u32[]{:S(2)}, u32[]{:S(2)}) %collective-permute-start.3) | collective-permute-done | bytes 196640 | tf_op jit(solution)/shard_map/ppermute | solution.py:21
  47.3 2.5 %keep_theirs.1.theirs_ref = bf16[8,256,1024]{2,1,0:T(8,128)(2,1)S(1)} custom-call(bf16[8,256,1024]{2,1,0:T(8,128)(2,1)} %collective-permute-done.in_ref), custom_call_target="tpu_custom_call" | custom-call | tf_op jit(solution)/shard_map/keep_theirs/pallas_call | solution.py:175
  53.9 2.9 %collective-permute-start.15 = (f32[96,96]{1,0:T(8,128)S(1)}, f32[96,96]{1,0:T(8,128)S(1)}, u32[]{:S(2)}, u32[]{:S(2)}) collective-permute-start(f32[96,96]{1,0:T(8,128)S(1)} %add.71), channel_id=1, source_target_pairs={{0,8},{1,9},{2,10},{3,11},{4,12},{5,13},{6,14},{7,15},{8,0},{9,1},... | collective-permute-start | bytes 110600 | tf_op jit(solution)/shard_map/ppermute | solution.py:21
  56.9 3.1 %collective-permute-done.15 = f32[96,96]{1,0:T(8,128)S(1)} collective-permute-done((f32[96,96]{1,0:T(8,128)S(1)}, f32[96,96]{1,0:T(8,128)S(1)}, u32[]{:S(2)}, u32[]{:S(2)}) %collective-permute-start.15) | collective-permute-done | bytes 36896 | tf_op jit(solution)/shard_map/ppermute | solution.py:21
  59.9 3.0 %shard_map.64.refs_0_ = f32[96,96]{1,0:T(8,128)S(1)} custom-call(f32[96,96]{1,0:T(8,128)S(1)} %add.72.gram_ref), custom_call_target="tpu_custom_call" | custom-call | tf_op jit(solution)/shard_map/pallas_call | solution.py:130
  66.8 3.9 %collective-permute-done.16 = f32[96,96]{1,0:T(8,128)S(1)} collective-permute-done((f32[96,96]{1,0:T(8,128)S(1)}, f32[96,96]{1,0:T(8,128)S(1)}, u32[]{:S(2)}, u32[]{:S(2)}) %collective-permute-start.16) | collective-permute-done | bytes 36896 | tf_op jit(solution)/shard_map/ppermute | solution.py:21
  72.1 3.9 %collective-permute-done.17 = f32[96,96]{1,0:T(8,128)S(1)} collective-permute-done((f32[96,96]{1,0:T(8,128)S(1)}, f32[96,96]{1,0:T(8,128)S(1)}, u32[]{:S(2)}, u32[]{:S(2)}) %collective-permute-start.17) | collective-permute-done | bytes 36896 | tf_op jit(solution)/shard_map/ppermute | solution.py:21
  81.3 3.0 %shard_map.66.inv_ref = f32[96,96]{1,0:T(8,128)S(1)} custom-call(f32[96,96]{1,0:T(8,128)S(1)} %add.75.gram_ref), custom_call_target="tpu_custom_call" | custom-call | tf_op jit(solution)/shard_map/pallas_call | solution.py:130
  85.6 2.9 %collective-permute-start.23 = (bf16[96,1024]{1,0:T(8,128)(2,1)S(1)}, bf16[96,1024]{1,0:T(8,128)(2,1)S(1)}, u32[]{:S(2)}, u32[]{:S(2)}) collective-permute-start(bf16[96,1024]{1,0:T(8,128)(2,1)S(1)} %add_convert_fusion.4), channel_id=1, source_target_pairs={{0,12},{1,13},{2,14},{3,15},{4,8},{5,9},{6,10},{7,11},{8,4},{9,5},... | collective-permute-start | bytes 589832 | tf_op jit(solution)/shard_map/ppermute | solution.py:21
  90.2 3.9 %collective-permute-done.23.refs_1_ = bf16[96,1024]{1,0:T(8,128)(2,1)S(1)} collective-permute-done((bf16[96,1024]{1,0:T(8,128)(2,1)S(1)}, bf16[96,1024]{1,0:T(8,128)(2,1)S(1)}, u32[]{:S(2)}, u32[]{:S(2)}) %collective-permute-start.23) | collective-permute-done | bytes 196640 | tf_op jit(solution)/shard_map/ppermute | solution.py:21
  94.1 6.9 %collective-permute-done.21.refs_0_ = bf16[96,1024]{1,0:T(8,128)(2,1)S(1)} collective-permute-done((bf16[96,1024]{1,0:T(8,128)(2,1)S(1)}, bf16[96,1024]{1,0:T(8,128)(2,1)S(1)}, u32[]{:S(2)}, u32[]{:S(2)}) %collective-permute-start.21) | collective-permute-done | bytes 196640 | tf_op jit(solution)/shard_map/ppermute | solution.py:21
  105.5 5.3 %collective-permute-done.30.refs_1_ = bf16[96,1024]{1,0:T(8,128)(2,1)S(1)} collective-permute-done((bf16[96,1024]{1,0:T(8,128)(2,1)S(1)}, bf16[96,1024]{1,0:T(8,128)(2,1)S(1)}, u32[]{:S(2)}, u32[]{:S(2)}) %collective-permute-start.30) | collective-permute-done | bytes 196640 | tf_op jit(solution)/shard_map/ppermute | solution.py:21
  111.1 2.5 %collective-permute-done.28.refs_2_ = bf16[96,1024]{1,0:T(8,128)(2,1)S(1)} collective-permute-done((bf16[96,1024]{1,0:T(8,128)(2,1)S(1)}, bf16[96,1024]{1,0:T(8,128)(2,1)S(1)}, u32[]{:S(2)}, u32[]{:S(2)}) %collective-permute-start.28) | collective-permute-done | bytes 196640 | tf_op jit(solution)/shard_map/ppermute | solution.py:21
  114.4 6.0 %collective-permute-done.26.refs_0_ = bf16[96,1024]{1,0:T(8,128)(2,1)S(1)} collective-permute-done((bf16[96,1024]{1,0:T(8,128)(2,1)S(1)}, bf16[96,1024]{1,0:T(8,128)(2,1)S(1)}, u32[]{:S(2)}, u32[]{:S(2)}) %collective-permute-start.26) | collective-permute-done | bytes 196640 | tf_op jit(solution)/shard_map/ppermute | solution.py:21
  130.7 2.7 %collective-permute-done.34 = f32[96,96]{1,0:T(8,128)S(1)} collective-permute-done((f32[96,96]{1,0:T(8,128)S(1)}, f32[96,96]{1,0:T(8,128)S(1)}, u32[]{:S(2)}, u32[]{:S(2)}) %collective-permute-start.34) | collective-permute-done | bytes 36896 | tf_op jit(solution)/shard_map/ppermute | solution.py:21
  134.9 3.5 %collective-permute-done.35 = f32[96,96]{1,0:T(8,128)S(1)} collective-permute-done((f32[96,96]{1,0:T(8,128)S(1)}, f32[96,96]{1,0:T(8,128)S(1)}, u32[]{:S(2)}, u32[]{:S(2)}) %collective-permute-start.35) | collective-permute-done | bytes 36896 | tf_op jit(solution)/shard_map/ppermute | solution.py:21
  144.1 3.0 %shard_map.75 = f32[96,96]{1,0:T(8,128)S(1)} custom-call(f32[96,96]{1,0:T(8,128)S(1)} %add.82.gram_ref), custom_call_target="tpu_custom_call" | custom-call | tf_op jit(solution)/shard_map/pallas_call | solution.py:130
  149.3 2.7 %collective-permute-start.41 = (bf16[96,1024]{1,0:T(8,128)(2,1)S(1)}, bf16[96,1024]{1,0:T(8,128)(2,1)S(1)}, u32[]{:S(2)}, u32[]{:S(2)}) collective-permute-start(bf16[96,1024]{1,0:T(8,128)(2,1)S(1)} %add_convert_fusion.1), channel_id=1, source_target_pairs={{0,12},{1,13},{2,14},{3,15},{4,8},{5,9},{6,10},{7,11},{8,4},{9,5},... | collective-permute-start | bytes 589832 | tf_op jit(solution)/shard_map/ppermute | solution.py:21
  155.0 6.1 %collective-permute-done.39 = bf16[96,1024]{1,0:T(8,128)(2,1)S(1)} collective-permute-done((bf16[96,1024]{1,0:T(8,128)(2,1)S(1)}, bf16[96,1024]{1,0:T(8,128)(2,1)S(1)}, u32[]{:S(2)}, u32[]{:S(2)}) %collective-permute-start.39) | collective-permute-done | bytes 196640 | tf_op jit(solution)/shard_map/ppermute | solution.py:21
  (121 shorter events, 67.4 us)
Async XLA Ops:
  4.9 41.7 %collective-permute-start = (bf16[8,256,1024]{2,1,0:T(8,128)(2,1)}, bf16[8,256,1024]{2,1,0:T(8,128)(2,1)}, u32[]{:S(2)}, u32[]{:S(2)}) collective-permute-start(bf16[8,256,1024]{2,1,0:T(8,128)(2,1)} %shard_map.60), channel_id=1, source_target_pairs={{0,1},{1,0},{2,3},{3,2},{4,5},{5,4},{6,7},{7,6},{8,9},{9,8},{10,11... | collective-permute-start | bytes 12582920 | tf_op jit(solution)/shard_map/ppermute | solution.py:21
  16.5 15.4 %collective-permute-start.7 = (bf16[96,1024]{1,0:T(8,128)(2,1)S(1)}, bf16[96,1024]{1,0:T(8,128)(2,1)S(1)}, u32[]{:S(2)}, u32[]{:S(2)}) collective-permute-start(bf16[96,1024]{1,0:T(8,128)(2,1)S(1)} %smooth.1.refs_0_), channel_id=1, source_target_pairs={{0,4},{1,5},{2,6},{3,7},{4,0},{5,1},{6,2},{7,3},{8,12},{9,13},{10,... | collective-permute-start | bytes 589832 | tf_op jit(solution)/shard_map/ppermute | solution.py:21
  21.4 12.5 %collective-permute-start.5 = (bf16[96,1024]{1,0:T(8,128)(2,1)S(1)}, bf16[96,1024]{1,0:T(8,128)(2,1)S(1)}, u32[]{:S(2)}, u32[]{:S(2)}) collective-permute-start(bf16[96,1024]{1,0:T(8,128)(2,1)S(1)} %smooth.1.refs_0_), channel_id=1, source_target_pairs={{0,12},{1,13},{2,14},{3,15},{4,8},{5,9},{6,10},{7,11},{8,4},{9,5},... | collective-permute-start | bytes 589832 | tf_op jit(solution)/shard_map/ppermute | solution.py:21
  23.9 18.4 %collective-permute-start.3 = (bf16[96,1024]{1,0:T(8,128)(2,1)S(1)}, bf16[96,1024]{1,0:T(8,128)(2,1)S(1)}, u32[]{:S(2)}, u32[]{:S(2)}) collective-permute-start(bf16[96,1024]{1,0:T(8,128)(2,1)S(1)} %smooth.1.refs_0_), channel_id=1, source_target_pairs={{0,8},{1,9},{2,10},{3,11},{4,12},{5,13},{6,14},{7,15},{8,0},{9,1},... | collective-permute-start | bytes 589832 | tf_op jit(solution)/shard_map/ppermute | solution.py:21
  30.1 19.7 %collective-permute-start.8 = (bf16[96,1024]{1,0:T(8,128)(2,1)S(1)}, bf16[96,1024]{1,0:T(8,128)(2,1)S(1)}, u32[]{:S(2)}, u32[]{:S(2)}) collective-permute-start(bf16[96,1024]{1,0:T(8,128)(2,1)S(1)} %smooth.1.refs_0_), channel_id=1, source_target_pairs={{0,2},{1,3},{2,0},{3,1},{4,6},{5,7},{6,4},{7,5},{8,10},{9,11},{10,... | collective-permute-start | bytes 589832 | tf_op jit(solution)/shard_map/ppermute | solution.py:21
  31.9 17.9 %collective-permute-start.9 = (bf16[96,1024]{1,0:T(8,128)(2,1)S(1)}, bf16[96,1024]{1,0:T(8,128)(2,1)S(1)}, u32[]{:S(2)}, u32[]{:S(2)}) collective-permute-start(bf16[96,1024]{1,0:T(8,128)(2,1)S(1)} %collective-permute-done.7.refs_1_), channel_id=1, source_target_pairs={{0,2},{1,3},{2,0},{3,1},{4,6},{5,7},{6,4},{7,5},{8,10},{9,11},{10,... | collective-permute-start | bytes 589832 | tf_op jit(solution)/shard_map/ppermute | solution.py:21
  34.0 17.9 %collective-permute-start.6 = (bf16[96,1024]{1,0:T(8,128)(2,1)S(1)}, bf16[96,1024]{1,0:T(8,128)(2,1)S(1)}, u32[]{:S(2)}, u32[]{:S(2)}) collective-permute-start(bf16[96,1024]{1,0:T(8,128)(2,1)S(1)} %collective-permute-done.5.refs_2_), channel_id=1, source_target_pairs={{0,2},{1,3},{2,0},{3,1},{4,6},{5,7},{6,4},{7,5},{8,10},{9,11},{10,... | collective-permute-start | bytes 589832 | tf_op jit(solution)/shard_map/ppermute | solution.py:21
  42.3 10.3 %collective-permute-start.4 = (bf16[96,1024]{1,0:T(8,128)(2,1)S(1)}, bf16[96,1024]{1,0:T(8,128)(2,1)S(1)}, u32[]{:S(2)}, u32[]{:S(2)}) collective-permute-start(bf16[96,1024]{1,0:T(8,128)(2,1)S(1)} %collective-permute-done.3.refs_0_), channel_id=1, source_target_pairs={{0,2},{1,3},{2,0},{3,1},{4,6},{5,7},{6,4},{7,5},{8,10},{9,11},{10,... | collective-permute-start | bytes 589832 | tf_op jit(solution)/shard_map/ppermute | solution.py:21
  53.1 9.9 %collective-permute-start.10 = (f32[96,512]{1,0:T(8,128)S(1)}, f32[96,512]{1,0:T(8,128)S(1)}, u32[]{:S(2)}, u32[]{:S(2)}) collective-permute-start(f32[96,512]{1,0:T(8,128)S(1)} %get-tuple-element.26), channel_id=1, source_target_pairs={{0,1},{1,0},{2,3},{3,2},{4,5},{5,4},{6,7},{7,6},{8,9},{9,8},{10,11... | collective-permute-start | bytes 589832 | tf_op jit(solution)/shard_map/ppermute | solution.py:21
  64.7 19.6 %collective-permute-start.24 = (bf16[96,1024]{1,0:T(8,128)(2,1)S(1)}, bf16[96,1024]{1,0:T(8,128)(2,1)S(1)}, u32[]{:S(2)}, u32[]{:S(2)}) collective-permute-start(bf16[96,1024]{1,0:T(8,128)(2,1)S(1)} %get-tuple-element.35), channel_id=1, source_target_pairs={{0,2},{1,3},{2,0},{3,1},{4,6},{5,7},{6,4},{7,5},{8,10},{9,11},{10,... | collective-permute-start | bytes 589832 | tf_op jit(solution)/shard_map/ppermute | solution.py:21
  79.8 10.2 %collective-permute-start.19 = (bf16[96,1024]{1,0:T(8,128)(2,1)S(1)}, bf16[96,1024]{1,0:T(8,128)(2,1)S(1)}, u32[]{:S(2)}, u32[]{:S(2)}) collective-permute-start(bf16[96,1024]{1,0:T(8,128)(2,1)S(1)} %get-tuple-element.30), channel_id=1, source_target_pairs={{0,2},{1,3},{2,0},{3,1},{4,6},{5,7},{6,4},{7,5},{8,10},{9,11},{10,... | collective-permute-start | bytes 589832 | tf_op jit(solution)/shard_map/ppermute | solution.py:21
  88.5 12.5 %collective-permute-start.21 = (bf16[96,1024]{1,0:T(8,128)(2,1)S(1)}, bf16[96,1024]{1,0:T(8,128)(2,1)S(1)}, u32[]{:S(2)}, u32[]{:S(2)}) collective-permute-start(bf16[96,1024]{1,0:T(8,128)(2,1)S(1)} %add_convert_fusion.5), channel_id=1, source_target_pairs={{0,8},{1,9},{2,10},{3,11},{4,12},{5,13},{6,14},{7,15},{8,0},{9,1},... | collective-permute-start | bytes 589832 | tf_op jit(solution)/shard_map/ppermute | solution.py:21
  101.5 9.3 %collective-permute-start.30 = (bf16[96,1024]{1,0:T(8,128)(2,1)S(1)}, bf16[96,1024]{1,0:T(8,128)(2,1)S(1)}, u32[]{:S(2)}, u32[]{:S(2)}) collective-permute-start(bf16[96,1024]{1,0:T(8,128)(2,1)S(1)} %shard_map.70.refs_0_), channel_id=1, source_target_pairs={{0,4},{1,5},{2,6},{3,7},{4,0},{5,1},{6,2},{7,3},{8,12},{9,13},{10,... | collective-permute-start | bytes 589832 | tf_op jit(solution)/shard_map/ppermute | solution.py:21
  101.6 12.0 %collective-permute-start.28 = (bf16[96,1024]{1,0:T(8,128)(2,1)S(1)}, bf16[96,1024]{1,0:T(8,128)(2,1)S(1)}, u32[]{:S(2)}, u32[]{:S(2)}) collective-permute-start(bf16[96,1024]{1,0:T(8,128)(2,1)S(1)} %shard_map.70.refs_0_), channel_id=1, source_target_pairs={{0,12},{1,13},{2,14},{3,15},{4,8},{5,9},{6,10},{7,11},{8,4},{9,5},... | collective-permute-start | bytes 589832 | tf_op jit(solution)/shard_map/ppermute | solution.py:21
  104.0 16.4 %collective-permute-start.26 = (bf16[96,1024]{1,0:T(8,128)(2,1)S(1)}, bf16[96,1024]{1,0:T(8,128)(2,1)S(1)}, u32[]{:S(2)}, u32[]{:S(2)}) collective-permute-start(bf16[96,1024]{1,0:T(8,128)(2,1)S(1)} %shard_map.70.refs_0_), channel_id=1, source_target_pairs={{0,8},{1,9},{2,10},{3,11},{4,12},{5,13},{6,14},{7,15},{8,0},{9,1},... | collective-permute-start | bytes 589832 | tf_op jit(solution)/shard_map/ppermute | solution.py:21
  105.1 15.9 %collective-permute-start.31 = (bf16[96,1024]{1,0:T(8,128)(2,1)S(1)}, bf16[96,1024]{1,0:T(8,128)(2,1)S(1)}, u32[]{:S(2)}, u32[]{:S(2)}) collective-permute-start(bf16[96,1024]{1,0:T(8,128)(2,1)S(1)} %shard_map.70.refs_0_), channel_id=1, source_target_pairs={{0,2},{1,3},{2,0},{3,1},{4,6},{5,7},{6,4},{7,5},{8,10},{9,11},{10,... | collective-permute-start | bytes 589832 | tf_op jit(solution)/shard_map/ppermute | solution.py:21
  110.8 10.2 %collective-permute-start.32 = (bf16[96,1024]{1,0:T(8,128)(2,1)S(1)}, bf16[96,1024]{1,0:T(8,128)(2,1)S(1)}, u32[]{:S(2)}, u32[]{:S(2)}) collective-permute-start(bf16[96,1024]{1,0:T(8,128)(2,1)S(1)} %collective-permute-done.30.refs_1_), channel_id=1, source_target_pairs={{0,2},{1,3},{2,0},{3,1},{4,6},{5,7},{6,4},{7,5},{8,10},{9,11},{10,... | collective-permute-start | bytes 589832 | tf_op jit(solution)/shard_map/ppermute | solution.py:21
  113.6 9.3 %collective-permute-start.29 = (bf16[96,1024]{1,0:T(8,128)(2,1)S(1)}, bf16[96,1024]{1,0:T(8,128)(2,1)S(1)}, u32[]{:S(2)}, u32[]{:S(2)}) collective-permute-start(bf16[96,1024]{1,0:T(8,128)(2,1)S(1)} %collective-permute-done.28.refs_2_), channel_id=1, source_target_pairs={{0,2},{1,3},{2,0},{3,1},{4,6},{5,7},{6,4},{7,5},{8,10},{9,11},{10,... | collective-permute-start | bytes 589832 | tf_op jit(solution)/shard_map/ppermute | solution.py:21
  128.6 18.5 %collective-permute-start.38 = (bf16[96,1024]{1,0:T(8,128)(2,1)S(1)}, bf16[96,1024]{1,0:T(8,128)(2,1)S(1)}, u32[]{:S(2)}, u32[]{:S(2)}) collective-permute-start(bf16[96,1024]{1,0:T(8,128)(2,1)S(1)} %shard_map.78), channel_id=1, source_target_pairs={{0,2},{1,3},{2,0},{3,1},{4,6},{5,7},{6,4},{7,5},{8,10},{9,11},{10,... | collective-permute-start | bytes 589832 | tf_op jit(solution)/shard_map/ppermute | solution.py:21
  142.1 10.6 %collective-permute-start.42 = (bf16[96,1024]{1,0:T(8,128)(2,1)S(1)}, bf16[96,1024]{1,0:T(8,128)(2,1)S(1)}, u32[]{:S(2)}, u32[]{:S(2)}) collective-permute-start(bf16[96,1024]{1,0:T(8,128)(2,1)S(1)} %get-tuple-element.47), channel_id=1, source_target_pairs={{0,2},{1,3},{2,0},{3,1},{4,6},{5,7},{6,4},{7,5},{8,10},{9,11},{10,... | collective-permute-start | bytes 589832 | tf_op jit(solution)/shard_map/ppermute | solution.py:21
  143.5 11.5 %collective-permute-start.37 = (bf16[96,1024]{1,0:T(8,128)(2,1)S(1)}, bf16[96,1024]{1,0:T(8,128)(2,1)S(1)}, u32[]{:S(2)}, u32[]{:S(2)}) collective-permute-start(bf16[96,1024]{1,0:T(8,128)(2,1)S(1)} %get-tuple-element.42), channel_id=1, source_target_pairs={{0,2},{1,3},{2,0},{3,1},{4,6},{5,7},{6,4},{7,5},{8,10},{9,11},{10,... | collective-permute-start | bytes 589832 | tf_op jit(solution)/shard_map/ppermute | solution.py:21
  147.2 13.9 %collective-permute-start.39 = (bf16[96,1024]{1,0:T(8,128)(2,1)S(1)}, bf16[96,1024]{1,0:T(8,128)(2,1)S(1)}, u32[]{:S(2)}, u32[]{:S(2)}) collective-permute-start(bf16[96,1024]{1,0:T(8,128)(2,1)S(1)} %add_convert_fusion.2), channel_id=1, source_target_pairs={{0,8},{1,9},{2,10},{3,11},{4,12},{5,13},{6,14},{7,15},{8,0},{9,1},... | collective-permute-start | bytes 589832 | tf_op jit(solution)/shard_map/ppermute | solution.py:21
  149.3 11.8 %collective-permute-start.41 = (bf16[96,1024]{1,0:T(8,128)(2,1)S(1)}, bf16[96,1024]{1,0:T(8,128)(2,1)S(1)}, u32[]{:S(2)}, u32[]{:S(2)}) collective-permute-start(bf16[96,1024]{1,0:T(8,128)(2,1)S(1)} %add_convert_fusion.1), channel_id=1, source_target_pairs={{0,12},{1,13},{2,14},{3,15},{4,8},{5,9},{6,10},{7,11},{8,4},{9,5},... | collective-permute-start | bytes 589832 | tf_op jit(solution)/shard_map/ppermute | solution.py:21
  152.7 9.5 %collective-permute-start.43 = (bf16[96,1024]{1,0:T(8,128)(2,1)S(1)}, bf16[96,1024]{1,0:T(8,128)(2,1)S(1)}, u32[]{:S(2)}, u32[]{:S(2)}) collective-permute-start(bf16[96,1024]{1,0:T(8,128)(2,1)S(1)} %add_convert_fusion), channel_id=1, source_target_pairs={{0,4},{1,5},{2,6},{3,7},{4,0},{5,1},{6,2},{7,3},{8,12},{9,13},{10,... | collective-permute-start | bytes 589832 | tf_op jit(solution)/shard_map/ppermute | solution.py:21
  (25 other events, 174.7 us)

commit v2 on v1

--- a/solution.py
+++ b/solution.py
@@ -82,14 +82,12 @@
     )(jnp.stack([top, bottom]).astype(jnp.int32), before, sketch, after)
 
 
-def inverse_kernel(total, gram_ref, out_ref, *, step=8):
-    size = gram_ref.shape[0]
-    groups = size // 8
+def eliminate(rows, out_ref, step=8):
+    groups, size = len(rows), rows[0].shape[1]
     shape = (8, size)
     lane = lax.broadcasted_iota(jnp.int32, shape, 1)
     sub = lax.broadcasted_iota(jnp.int32, shape, 0)
     full = lambda v: jnp.broadcast_to(v, shape)
-    rows = [gram_ref[8 * g:8 * g + 8, :] * (1.0 / total) for g in range(groups)]
     scale = [None] * groups
     for j in range(0, size, step):
         g, s = j // 8, j % 8
@@ -124,6 +122,11 @@
         out_ref[8 * g:8 * g + 8, :] = lower * scale[g]
 
 
+def inverse_kernel(total, gram_ref, out_ref):
+    size = gram_ref.shape[0]
+    eliminate([gram_ref[g:g + 8, :] * (1.0 / total) for g in range(0, size, 8)], out_ref)
+
+
 def small_call(kernel, outs, args, smem=0, scratch=()):
     spaces = [pltpu.SMEM] * smem + [VM] * (len(args) - smem)
     many = isinstance(outs, list)
@@ -183,49 +186,54 @@
     )(x)
 
 
-def forward_kernel(slots, seeded, last, chip_ref, mine_ref, theirs_ref, *refs):
+def forward_kernel(slots, seeded, last, whiten, chip_ref, mine_ref, theirs_ref, *refs):
     parts, rest = refs[:len(slots)], refs[len(slots):]
-    rows = mine_ref.shape[1]
-    a = rest[0][:, :rows] if seeded else 0.0
-    b = rest[0][:, rows:] if seeded else 0.0
+    rows, columns = mine_ref.shape[1], parts[0].shape[0]
+    take = (pl.ds(0, rows), pl.ds(rows, rows), pl.ds(2 * rows, columns))[:2 + whiten]
+    sums = [rest[0][:, t] if seeded else 0.0 for t in take]
     for slot, part_ref in zip(slots, parts):
         m = chip_ref[0] ^ slot
         part = part_ref[...]
-        a += lax.dot_general(part, mine_ref[m], NT, preferred_element_type=f32)
-        b += lax.dot_general(part, theirs_ref[m], NT, preferred_element_type=f32)
-    out_ref = rest[1 if seeded else 0]
-    out_ref[:, :rows] = a
-    out_ref[:, rows:] = b
+        for i, other in enumerate((mine_ref[m], theirs_ref[m], part)[:len(take)]):
+            sums[i] += lax.dot_general(part, other, NT, preferred_element_type=f32)
+    outs = [(rest[1 if seeded else 0], sums)]
     if last:
-        rest[-1][:, :rows] = b
-        rest[-1][:, rows:] = a
-
-
-def forward_call(chip, mine, theirs, stage, seed, last):
+        outs.append((rest[-1], [sums[1], sums[0]] + sums[2:]))
+    for ref, values in outs:
+        for t, v in zip(take, values):
+            ref[:, t] = v
+
+
+def forward_call(chip, mine, theirs, stage, seed, last, whiten):
     slots, parts = [s for s, _ in stage], [p for _, p in stage]
     seeds = [] if seed is None else [seed]
-    shape = jax.ShapeDtypeStruct((parts[0].shape[0], 2 * mine.shape[1]), f32)
-    return small_call(functools.partial(forward_kernel, slots, seed is not None, last),
+    columns, width = parts[0].shape[0], 2 * mine.shape[1]
+    if whiten:
+        width += -(-columns // 128) * 128
+    shape = jax.ShapeDtypeStruct((columns, width), f32)
+    return small_call(functools.partial(forward_kernel, slots, seed is not None, last, whiten),
                       [shape, shape] if last else shape, [chip[None], mine, theirs] + parts + seeds,
                       smem=1)
 
 
-def finish_kernel(whitened, total_ref, other_ref, weights_ref, *refs):
-    y = (total_ref[...] + other_ref[...]) * weights_ref[...]
-    if whitened:
-        y = jnp.dot(refs[0][...], y, precision=HIGH, preferred_element_type=f32)
-    y_ref, weighted_ref, gram_ref = refs[-3:]
+def finish_kernel(params, total_ref, other_ref, weights_ref, y_ref, weighted_ref, gram_ref, *scratch):
+    width, columns = y_ref.shape[1], y_ref.shape[0]
+    y = (total_ref[:, :width] + other_ref[:, :width]) * weights_ref[...]
+    if params:
+        at = lambda g: (pl.ds(g, 8), pl.ds(width, columns))
+        eliminate([(total_ref[at(g)] + other_ref[at(g)]) * (1.0 / params) for g in range(0, columns, 8)], scratch[0])
+        y = jnp.dot(scratch[0][...], y, precision=HIGH, preferred_element_type=f32)
     y_ref[...] = y
     weighted_ref[...] = (y * weights_ref[...]).astype(bf16)
     gram_ref[...] = lax.dot_general(y, y, NT, precision=HIGH, preferred_element_type=f32)
 
 
-def finish(total, other, weights, white):
-    columns = total.shape[0]
-    outs = [jax.ShapeDtypeStruct(total.shape, f32), jax.ShapeDtypeStruct(total.shape, bf16),
+def finish(total, other, weights, params):
+    columns, width = total.shape[0], weights.shape[1]
+    outs = [jax.ShapeDtypeStruct((columns, width), f32), jax.ShapeDtypeStruct((columns, width), bf16),
             jax.ShapeDtypeStruct((columns, columns), f32)]
-    return small_call(functools.partial(finish_kernel, white is not None), outs,
-                      [total, other, weights] + ([] if white is None else [white]))
+    return small_call(functools.partial(finish_kernel, params), outs, [total, other, weights],
+                      scratch=[VM((columns, columns), f32)] if params else [])
 
 
 def backward_kernel(slots, chip_ref, mine_ref, theirs_ref, y_ref, *outs):
@@ -250,14 +258,36 @@
     refs[-1][...] = (jnp.dot(inv_ref[...], total, precision=HIGH, preferred_element_type=f32) * scale).astype(bf16)
 
 
+def project_kernel(scale, inv_ref, own_ref, *refs):
+    total = own_ref[...]
+    for r in refs[:-1]:
+        total = total + r[...].astype(f32)
+    out = jnp.dot(inv_ref[...], total, precision=HIGH, preferred_element_type=f32) * scale
+    length, _, strike = refs[-1].shape
+    for i in range(length):
+        refs[-1][i] = out[:, i * strike:(i + 1) * strike]
+
+
 def order(chips):
     return [0, 2, 6, 4] if chips == 8 else [2 * k for k in range(chips // 2)]
 
 
-def gram_sum(x, steps):
-    for k in steps:
-        x = x + swap(x, k)
-    return x
+def direct(n):
+    return n <= 16 and n & (n - 1) == 0
+
+
+def same_core():
+    n = lax.axis_size("row")
+    return [list(range(core, n, 2)) for core in range(2)]
+
+
+def gram_sum(x):
+    n = lax.axis_size("row")
+    if not direct(n):
+        return lax.psum(x, "row", axis_index_groups=same_core())
+    far = [swap(x, 4 * k) for k in range(1, n // 4)]
+    x = sum(far, x)
+    return x + swap(x, 2)
 
 
 def local(greens, track_id, sigma_inv, sketch):
@@ -267,7 +297,6 @@
     columns, length, strike = sketch.shape
     block = params // n
     total_rows = rows * n
-    row_scale = 1.0 / jnp.sqrt(f32(total_rows))
     me = lax.axis_index("row")
     core, chip = me % 2, me // 2
 
@@ -284,7 +313,12 @@
     theirs = keep(theirs)
     mine = pick(pltpu.with_memory_space_constraint(greens, pltpu.HBM), core, chips, block, VM)
 
-    def forward(own):
+    def forward(own, whiten):
+        if not direct(n):
+            parts = lax.all_gather(own, "row", axis_index_groups=same_core())
+            stage = [(m, parts[m]) for m in range(chips)]
+            total = forward_call(0 * chip, mine, theirs, stage, None, True, whiten)
+            return total[0], swap(total[1], 1)
         near, ks = {}, order(chips)
         for k in ks:
             near[k] = own if k == 0 else swap(own, 2 * k)
@@ -294,10 +328,13 @@
                   [(ks[-1] + 1, across[ks[-1]])]]
         total = None
         for i, stage in enumerate(stages):
-            total = forward_call(chip, mine, theirs, stage, total, i == len(stages) - 1)
+            total = forward_call(chip, mine, theirs, stage, total, i == len(stages) - 1, whiten)
         return total[0], swap(total[1], 1)
 
     def backward(weighted):
+        if not direct(n):
+            every = backward_call(0 * chip, mine, theirs, weighted, list(range(chips)), f32)
+            return [lax.psum_scatter(jnp.stack(every), "row", axis_index_groups=same_core())]
         ks = order(chips)[::-1]
 
         def call(slots, dtype):
@@ -309,21 +346,18 @@
         far = [swap(v.astype(bf16), 2 * k) for v, k in zip(sums, ks) if k]
         return [sums[-1]] + far
 
-    slower = [1 << i for i in range(2, n.bit_length() - 1)]
-    gram0 = gram_sum(lax.dot_general(omega, omega, NT, preferred_element_type=f32), [1, 2] + slower)
-    white = inverse_factor(gram0, params)
-    _, weighted, gram = finish(*forward(omega), weights, white)
+    _, weighted, gram = finish(*forward(omega, True), weights, float(params))
     pieces = backward(weighted)
-    inv_one = inverse_factor(gram_sum(gram, slower + [2]), total_rows)
+    inv_one = inverse_factor(gram_sum(gram), total_rows)
     back = small_call(functools.partial(back_kernel, float(total_rows) ** -0.5),
                       jax.ShapeDtypeStruct((columns, block), bf16), [inv_one] + pieces)
-    second, weighted, gram = finish(*forward(back), weights, None)
+    second, weighted, gram = finish(*forward(back, False), weights, None)
     pieces = backward(weighted)
-    inv_two = inverse_factor(gram_sum(gram, slower + [2]), total_rows)
-    projected = sum([v.astype(f32) for v in pieces[1:]], pieces[0])
+    inv_two = inverse_factor(gram_sum(gram), total_rows)
     range_basis = lax.dot_general(second[:, :rows], inv_two, (((0,), (1,)), ((), ())), precision=HIGH)
-    coefficients = lax.dot_general(projected, inv_two, (((0,), (1,)), ((), ())), precision=HIGH) * row_scale
-    return (range_basis, coefficients.reshape(length, strike, columns))
+    coefficients = small_call(functools.partial(project_kernel, float(total_rows) ** -0.5),
+                              jax.ShapeDtypeStruct((length, columns, strike), f32), [inv_two] + pieces)
+    return (range_basis, coefficients.transpose(0, 2, 1))
 
 
 def solution(mesh):

time: 164 us -> 165 us (level)
  waiting for transfers between devices: 73.2 us -> 80.5 us
  starting transfers between devices: 50.7 us -> 44.2 us
    ppermute x42 -> x40, waiting for transfers between devices: 69.2 us -> 76.5 us  [swap(): return lax.ppermute(x, 'row', [(i, i ^ k) for i in range(n)])]
    ppermute x42 -> x40, starting transfers between devices: 47.5 us -> 41 us  [swap(): return lax.ppermute(x, 'row', [(i, i ^ k) for i in range(n)])]
    pallas_call x18, Pallas kernels: 20.6 us -> 22.3 us  [small_call(): pl.pallas_call(kernel, out_shape=outs, in_specs=[pl.BlockSpec(memory_spac...]
  transfers between devices with their start and end apart: 44 -> 42, of which waited for: 25 -> 26; matrix products, arithmetic and copies ran while one was open for 1% -> 1% of each run, Pallas kernels for 16% -> 14%
where the time goes in v2:
time: 165 us
  waiting for transfers between devices  80.5 us (49%)
  starting transfers between devices  44.2 us (27%)
  Pallas kernels  34.7 us (21%)
  local copies, waits for them, and re-layouts  3.2 us (2%)
    ppermute x40, waiting for transfers between devices, swap(): return lax.ppermute(x, 'row', [(i, i ^ k) for i in range(n)])  76.5 us
    ppermute x40, starting transfers between devices, swap(): return lax.ppermute(x, 'row', [(i, i ^ k) for i in range(n)])  41 us
    pallas_call x18, Pallas kernels, small_call(): pl.pallas_call(kernel, out_shape=outs, in_specs=[pl.BlockSpec(memory_spac...  22.3 us
    pallas_call x2, Pallas kernels, pick(): pl.pallas_call(pick_kernel, out_shape=out((chips, greens.shape[0], block)...  6.49 us
    ppermute x1, waiting for transfers between devices, halo_rows(): before.insert(0, lax.ppermute(x[:, length - take:], 'row', up))  3.87 us
    pallas_call x1, Pallas kernels, smooth(): pl.pallas_call(smooth_kernel, out_shape=jax.ShapeDtypeStruct((columns, le...  3.54 us
  transfers between devices with their start and end apart: 42, of which 26 were waited for; matrix products, arithmetic and copies ran while one was open for 1% of the time, Pallas kernels for 14%

profile of v2, /device:TPU:0, one launch (start us, length us, event | category | flops | bytes accessed | tf_op | source)
XLA Modules:
  0.0 165.2 jit_solution(5922274479839901419)
XLA Ops:
  0.7 4.3 %shard_map.60 = bf16[8,256,1024]{2,1,0:T(8,128)(2,1)} custom-call(s32[1]{0:T(128)} %bitcast.2.core_ref, bf16[256,16384]{1,0:T(8,128)(2,1)} %in_ref.3), custom_call_target="tpu_custom_call" | custom-call | tf_op jit(solution)/shard_map/pallas_call | solution.py:163
  8.9 3.9 %collective-permute-done.1.before_ref = f32[96,4,128]{2,1,0:T(4,128)S(1)} collective-permute-done((f32[96,4,128]{2,1,0:T(4,128)S(1)}, f32[96,4,128]{2,1,0:T(4,128)S(1)}, u32[]{:S(2)}, u32[]{:S(2)}) %collective-permute-start.1) | collective-permute-done | bytes 196640 | tf_op jit(solution)/shard_map/ppermute | solution.py:32
  13.0 3.5 %smooth.1.refs_0_ = bf16[96,1024]{1,0:T(8,128)(2,1)S(1)} custom-call(s32[2]{0:T(128)S(1)} %pad_add_fusion.edge_ref, f32[96,4,128]{2,1,0:T(4,128)S(1)} %collective-permute-done.1.before_ref, f32[96,8,128]{2,1,0:T(8,128)S(1)} %copy-done.3, f32[96,4,128]{2,1,0:T(4,128)S(1)} %collective-permute-done.2.after_ref), custom_call_target="tpu_custom_call" | custom-call | tf_op jit(solution)/shard_map/smooth/pallas_call | solution.py:75
  16.5 4.9 %collective-permute-start.7 = (bf16[96,1024]{1,0:T(8,128)(2,1)S(1)}, bf16[96,1024]{1,0:T(8,128)(2,1)S(1)}, u32[]{:S(2)}, u32[]{:S(2)}) collective-permute-start(bf16[96,1024]{1,0:T(8,128)(2,1)S(1)} %smooth.1.refs_0_), channel_id=1, source_target_pairs={{0,4},{1,5},{2,6},{3,7},{4,0},{5,1},{6,2},{7,3},{8,12},{9,13},{10,... | collective-permute-start | bytes 589832 | tf_op jit(solution)/shard_map/ppermute | solution.py:21
  21.4 2.5 %collective-permute-start.5 = (bf16[96,1024]{1,0:T(8,128)(2,1)S(1)}, bf16[96,1024]{1,0:T(8,128)(2,1)S(1)}, u32[]{:S(2)}, u32[]{:S(2)}) collective-permute-start(bf16[96,1024]{1,0:T(8,128)(2,1)S(1)} %smooth.1.refs_0_), channel_id=1, source_target_pairs={{0,12},{1,13},{2,14},{3,15},{4,8},{5,9},{6,10},{7,11},{8,4},{9,5},... | collective-permute-start | bytes 589832 | tf_op jit(solution)/shard_map/ppermute | solution.py:21
  26.8 7.2 %collective-permute-done.5.refs_2_ = bf16[96,1024]{1,0:T(8,128)(2,1)S(1)} collective-permute-done((bf16[96,1024]{1,0:T(8,128)(2,1)S(1)}, bf16[96,1024]{1,0:T(8,128)(2,1)S(1)}, u32[]{:S(2)}, u32[]{:S(2)}) %collective-permute-start.5) | collective-permute-done | bytes 196640 | tf_op jit(solution)/shard_map/ppermute | solution.py:21
  33.9 8.4 %collective-permute-done.3.refs_0_ = bf16[96,1024]{1,0:T(8,128)(2,1)S(1)} collective-permute-done((bf16[96,1024]{1,0:T(8,128)(2,1)S(1)}, bf16[96,1024]{1,0:T(8,128)(2,1)S(1)}, u32[]{:S(2)}, u32[]{:S(2)}) %collective-permute-start.3) | collective-permute-done | bytes 196640 | tf_op jit(solution)/shard_map/ppermute | solution.py:21
  46.6 2.4 %keep_theirs.1.theirs_ref = bf16[8,256,1024]{2,1,0:T(8,128)(2,1)S(1)} custom-call(bf16[8,256,1024]{2,1,0:T(8,128)(2,1)} %collective-permute-done.in_ref), custom_call_target="tpu_custom_call" | custom-call | tf_op jit(solution)/shard_map/keep_theirs/pallas_call | solution.py:178
  55.2 4.2 %shard_map.64 = (f32[96,512]{1,0:T(8,128)}, bf16[96,512]{1,0:T(8,128)(2,1)S(1)}, f32[96,96]{1,0:T(8,128)S(1)}) custom-call(f32[96,640]{1,0:T(8,128)S(1)} %get-tuple-element.25.total_ref, f32[96,640]{1,0:T(8,128)S(1)} %collective-permute-done.10.other_ref, f32[1,512]{1,0:T(1,128)S(1)} %bitcast.12), custom_call_target="tpu_custom_call" | custom-call | tf_op jit(solution)/shard_map/pallas_call | solution.py:133
  59.9 3.4 %collective-permute-start.13 = (f32[96,96]{1,0:T(8,128)S(1)}, f32[96,96]{1,0:T(8,128)S(1)}, u32[]{:S(2)}, u32[]{:S(2)}) collective-permute-start(f32[96,96]{1,0:T(8,128)S(1)} %get-tuple-element.27), channel_id=1, source_target_pairs={{0,8},{1,9},{2,10},{3,11},{4,12},{5,13},{6,14},{7,15},{8,0},{9,1},... | collective-permute-start | bytes 110600 | tf_op jit(solution)/shard_map/ppermute | solution.py:21
  66.5 2.6 %collective-permute-done.14 = f32[96,96]{1,0:T(8,128)S(1)} collective-permute-done((f32[96,96]{1,0:T(8,128)S(1)}, f32[96,96]{1,0:T(8,128)S(1)}, u32[]{:S(2)}, u32[]{:S(2)}) %collective-permute-start.14) | collective-permute-done | bytes 36896 | tf_op jit(solution)/shard_map/ppermute | solution.py:21
  74.5 3.0 %shard_map.65.inv_ref = f32[96,96]{1,0:T(8,128)S(1)} custom-call(f32[96,96]{1,0:T(8,128)S(1)} %add.57.gram_ref), custom_call_target="tpu_custom_call" | custom-call | tf_op jit(solution)/shard_map/pallas_call | solution.py:133
  80.8 2.9 %collective-permute-done.17 = bf16[96,1024]{1,0:T(8,128)(2,1)S(1)} collective-permute-done((bf16[96,1024]{1,0:T(8,128)(2,1)S(1)}, bf16[96,1024]{1,0:T(8,128)(2,1)S(1)}, u32[]{:S(2)}, u32[]{:S(2)}) %collective-permute-start.17) | collective-permute-done | bytes 196640 | tf_op jit(solution)/shard_map/ppermute | solution.py:21
  85.9 3.3 %collective-permute-done.20.refs_1_ = bf16[96,1024]{1,0:T(8,128)(2,1)S(1)} collective-permute-done((bf16[96,1024]{1,0:T(8,128)(2,1)S(1)}, bf16[96,1024]{1,0:T(8,128)(2,1)S(1)}, u32[]{:S(2)}, u32[]{:S(2)}) %collective-permute-start.20) | collective-permute-done | bytes 196640 | tf_op jit(solution)/shard_map/ppermute | solution.py:21
  89.3 7.0 %collective-permute-done.18.refs_0_ = bf16[96,1024]{1,0:T(8,128)(2,1)S(1)} collective-permute-done((bf16[96,1024]{1,0:T(8,128)(2,1)S(1)}, bf16[96,1024]{1,0:T(8,128)(2,1)S(1)}, u32[]{:S(2)}, u32[]{:S(2)}) %collective-permute-start.18) | collective-permute-done | bytes 196640 | tf_op jit(solution)/shard_map/ppermute | solution.py:21
  101.3 5.3 %collective-permute-done.27.refs_1_ = bf16[96,1024]{1,0:T(8,128)(2,1)S(1)} collective-permute-done((bf16[96,1024]{1,0:T(8,128)(2,1)S(1)}, bf16[96,1024]{1,0:T(8,128)(2,1)S(1)}, u32[]{:S(2)}, u32[]{:S(2)}) %collective-permute-start.27) | collective-permute-done | bytes 196640 | tf_op jit(solution)/shard_map/ppermute | solution.py:21
  106.7 2.2 %collective-permute-done.25.refs_2_ = bf16[96,1024]{1,0:T(8,128)(2,1)S(1)} collective-permute-done((bf16[96,1024]{1,0:T(8,128)(2,1)S(1)}, bf16[96,1024]{1,0:T(8,128)(2,1)S(1)}, u32[]{:S(2)}, u32[]{:S(2)}) %collective-permute-start.25) | collective-permute-done | bytes 196640 | tf_op jit(solution)/shard_map/ppermute | solution.py:21
  109.9 5.8 %collective-permute-done.23.refs_0_ = bf16[96,1024]{1,0:T(8,128)(2,1)S(1)} collective-permute-done((bf16[96,1024]{1,0:T(8,128)(2,1)S(1)}, bf16[96,1024]{1,0:T(8,128)(2,1)S(1)}, u32[]{:S(2)}, u32[]{:S(2)}) %collective-permute-start.23) | collective-permute-done | bytes 196640 | tf_op jit(solution)/shard_map/ppermute | solution.py:21
  128.2 3.6 %collective-permute-done.32 = f32[96,96]{1,0:T(8,128)S(1)} collective-permute-done((f32[96,96]{1,0:T(8,128)S(1)}, f32[96,96]{1,0:T(8,128)S(1)}, u32[]{:S(2)}, u32[]{:S(2)}) %collective-permute-start.32) | collective-permute-done | bytes 36896 | tf_op jit(solution)/shard_map/ppermute | solution.py:21
  139.7 3.0 %shard_map.74.inv_ref = f32[96,96]{1,0:T(8,128)S(1)} custom-call(f32[96,96]{1,0:T(8,128)S(1)} %add.65.gram_ref), custom_call_target="tpu_custom_call" | custom-call | tf_op jit(solution)/shard_map/pallas_call | solution.py:133
  143.7 3.9 %collective-permute-done.38 = bf16[96,1024]{1,0:T(8,128)(2,1)S(1)} collective-permute-done((bf16[96,1024]{1,0:T(8,128)(2,1)S(1)}, bf16[96,1024]{1,0:T(8,128)(2,1)S(1)}, u32[]{:S(2)}, u32[]{:S(2)}) %collective-permute-start.38) | collective-permute-done | bytes 196640 | tf_op jit(solution)/shard_map/ppermute | solution.py:21
  149.2 2.4 %collective-permute-done.36 = bf16[96,1024]{1,0:T(8,128)(2,1)S(1)} collective-permute-done((bf16[96,1024]{1,0:T(8,128)(2,1)S(1)}, bf16[96,1024]{1,0:T(8,128)(2,1)S(1)}, u32[]{:S(2)}, u32[]{:S(2)}) %collective-permute-start.36) | collective-permute-done | bytes 196640 | tf_op jit(solution)/shard_map/ppermute | solution.py:21
  153.8 2.3 %collective-permute-done.39.refs_1_ = bf16[96,1024]{1,0:T(8,128)(2,1)S(1)} collective-permute-done((bf16[96,1024]{1,0:T(8,128)(2,1)S(1)}, bf16[96,1024]{1,0:T(8,128)(2,1)S(1)}, u32[]{:S(2)}, u32[]{:S(2)}) %collective-permute-start.39) | collective-permute-done | bytes 196640 | tf_op jit(solution)/shard_map/ppermute | solution.py:21
  156.0 7.8 %collective-permute-done.37.refs_0_ = bf16[96,1024]{1,0:T(8,128)(2,1)S(1)} collective-permute-done((bf16[96,1024]{1,0:T(8,128)(2,1)S(1)}, bf16[96,1024]{1,0:T(8,128)(2,1)S(1)}, u32[]{:S(2)}, u32[]{:S(2)}) %collective-permute-start.37) | collective-permute-done | bytes 196640 | tf_op jit(solution)/shard_map/ppermute | solution.py:21
  (109 shorter events, 64.3 us)
Async XLA Ops:
  4.9 41.7 %collective-permute-start = (bf16[8,256,1024]{2,1,0:T(8,128)(2,1)}, bf16[8,256,1024]{2,1,0:T(8,128)(2,1)}, u32[]{:S(2)}, u32[]{:S(2)}) collective-permute-start(bf16[8,256,1024]{2,1,0:T(8,128)(2,1)} %shard_map.60), channel_id=1, source_target_pairs={{0,1},{1,0},{2,3},{3,2},{4,5},{5,4},{6,7},{7,6},{8,9},{9,8},{10,11... | collective-permute-start | bytes 12582920 | tf_op jit(solution)/shard_map/ppermute | solution.py:21
  16.5 10.3 %collective-permute-start.7 = (bf16[96,1024]{1,0:T(8,128)(2,1)S(1)}, bf16[96,1024]{1,0:T(8,128)(2,1)S(1)}, u32[]{:S(2)}, u32[]{:S(2)}) collective-permute-start(bf16[96,1024]{1,0:T(8,128)(2,1)S(1)} %smooth.1.refs_0_), channel_id=1, source_target_pairs={{0,4},{1,5},{2,6},{3,7},{4,0},{5,1},{6,2},{7,3},{8,12},{9,13},{10,... | collective-permute-start | bytes 589832 | tf_op jit(solution)/shard_map/ppermute | solution.py:21
  21.4 12.5 %collective-permute-start.5 = (bf16[96,1024]{1,0:T(8,128)(2,1)S(1)}, bf16[96,1024]{1,0:T(8,128)(2,1)S(1)}, u32[]{:S(2)}, u32[]{:S(2)}) collective-permute-start(bf16[96,1024]{1,0:T(8,128)(2,1)S(1)} %smooth.1.refs_0_), channel_id=1, source_target_pairs={{0,12},{1,13},{2,14},{3,15},{4,8},{5,9},{6,10},{7,11},{8,4},{9,5},... | collective-permute-start | bytes 589832 | tf_op jit(solution)/shard_map/ppermute | solution.py:21
  23.9 18.4 %collective-permute-start.3 = (bf16[96,1024]{1,0:T(8,128)(2,1)S(1)}, bf16[96,1024]{1,0:T(8,128)(2,1)S(1)}, u32[]{:S(2)}, u32[]{:S(2)}) collective-permute-start(bf16[96,1024]{1,0:T(8,128)(2,1)S(1)} %smooth.1.refs_0_), channel_id=1, source_target_pairs={{0,8},{1,9},{2,10},{3,11},{4,12},{5,13},{6,14},{7,15},{8,0},{9,1},... | collective-permute-start | bytes 589832 | tf_op jit(solution)/shard_map/ppermute | solution.py:21
  24.0 25.0 %collective-permute-start.8 = (bf16[96,1024]{1,0:T(8,128)(2,1)S(1)}, bf16[96,1024]{1,0:T(8,128)(2,1)S(1)}, u32[]{:S(2)}, u32[]{:S(2)}) collective-permute-start(bf16[96,1024]{1,0:T(8,128)(2,1)S(1)} %smooth.1.refs_0_), channel_id=1, source_target_pairs={{0,2},{1,3},{2,0},{3,1},{4,6},{5,7},{6,4},{7,5},{8,10},{9,11},{10,... | collective-permute-start | bytes 589832 | tf_op jit(solution)/shard_map/ppermute | solution.py:21
  26.8 22.2 %collective-permute-start.9 = (bf16[96,1024]{1,0:T(8,128)(2,1)S(1)}, bf16[96,1024]{1,0:T(8,128)(2,1)S(1)}, u32[]{:S(2)}, u32[]{:S(2)}) collective-permute-start(bf16[96,1024]{1,0:T(8,128)(2,1)S(1)} %collective-permute-done.7.refs_1_), channel_id=1, source_target_pairs={{0,2},{1,3},{2,0},{3,1},{4,6},{5,7},{6,4},{7,5},{8,10},{9,11},{10,... | collective-permute-start | bytes 589832 | tf_op jit(solution)/shard_map/ppermute | solution.py:21
  33.9 18.1 %collective-permute-start.6 = (bf16[96,1024]{1,0:T(8,128)(2,1)S(1)}, bf16[96,1024]{1,0:T(8,128)(2,1)S(1)}, u32[]{:S(2)}, u32[]{:S(2)}) collective-permute-start(bf16[96,1024]{1,0:T(8,128)(2,1)S(1)} %collective-permute-done.5.refs_2_), channel_id=1, source_target_pairs={{0,2},{1,3},{2,0},{3,1},{4,6},{5,7},{6,4},{7,5},{8,10},{9,11},{10,... | collective-permute-start | bytes 589832 | tf_op jit(solution)/shard_map/ppermute | solution.py:21
  42.3 10.6 %collective-permute-start.4 = (bf16[96,1024]{1,0:T(8,128)(2,1)S(1)}, bf16[96,1024]{1,0:T(8,128)(2,1)S(1)}, u32[]{:S(2)}, u32[]{:S(2)}) collective-permute-start(bf16[96,1024]{1,0:T(8,128)(2,1)S(1)} %collective-permute-done.3.refs_0_), channel_id=1, source_target_pairs={{0,2},{1,3},{2,0},{3,1},{4,6},{5,7},{6,4},{7,5},{8,10},{9,11},{10,... | collective-permute-start | bytes 589832 | tf_op jit(solution)/shard_map/ppermute | solution.py:21
  64.4 13.1 %collective-permute-start.21 = (bf16[96,1024]{1,0:T(8,128)(2,1)S(1)}, bf16[96,1024]{1,0:T(8,128)(2,1)S(1)}, u32[]{:S(2)}, u32[]{:S(2)}) collective-permute-start(bf16[96,1024]{1,0:T(8,128)(2,1)S(1)} %get-tuple-element.35), channel_id=1, source_target_pairs={{0,2},{1,3},{2,0},{3,1},{4,6},{5,7},{6,4},{7,5},{8,10},{9,11},{10,... | collective-permute-start | bytes 589832 | tf_op jit(solution)/shard_map/ppermute | solution.py:21
  72.4 11.3 %collective-permute-start.17 = (bf16[96,1024]{1,0:T(8,128)(2,1)S(1)}, bf16[96,1024]{1,0:T(8,128)(2,1)S(1)}, u32[]{:S(2)}, u32[]{:S(2)}) collective-permute-start(bf16[96,1024]{1,0:T(8,128)(2,1)S(1)} %shard_map.68), channel_id=1, source_target_pairs={{0,2},{1,3},{2,0},{3,1},{4,6},{5,7},{6,4},{7,5},{8,10},{9,11},{10,... | collective-permute-start | bytes 589832 | tf_op jit(solution)/shard_map/ppermute | solution.py:21
  73.7 12.1 %collective-permute-start.16 = (bf16[96,1024]{1,0:T(8,128)(2,1)S(1)}, bf16[96,1024]{1,0:T(8,128)(2,1)S(1)}, u32[]{:S(2)}, u32[]{:S(2)}) collective-permute-start(bf16[96,1024]{1,0:T(8,128)(2,1)S(1)} %get-tuple-element.30), channel_id=1, source_target_pairs={{0,2},{1,3},{2,0},{3,1},{4,6},{5,7},{6,4},{7,5},{8,10},{9,11},{10,... | collective-permute-start | bytes 589832 | tf_op jit(solution)/shard_map/ppermute | solution.py:21
  79.5 9.8 %collective-permute-start.20 = (bf16[96,1024]{1,0:T(8,128)(2,1)S(1)}, bf16[96,1024]{1,0:T(8,128)(2,1)S(1)}, u32[]{:S(2)}, u32[]{:S(2)}) collective-permute-start(bf16[96,1024]{1,0:T(8,128)(2,1)S(1)} %add_convert_fusion.4), channel_id=1, source_target_pairs={{0,12},{1,13},{2,14},{3,15},{4,8},{5,9},{6,10},{7,11},{8,4},{9,5},... | collective-permute-start | bytes 589832 | tf_op jit(solution)/shard_map/ppermute | solution.py:21
  83.7 12.6 %collective-permute-start.18 = (bf16[96,1024]{1,0:T(8,128)(2,1)S(1)}, bf16[96,1024]{1,0:T(8,128)(2,1)S(1)}, u32[]{:S(2)}, u32[]{:S(2)}) collective-permute-start(bf16[96,1024]{1,0:T(8,128)(2,1)S(1)} %add_convert_fusion.5), channel_id=1, source_target_pairs={{0,8},{1,9},{2,10},{3,11},{4,12},{5,13},{6,14},{7,15},{8,0},{9,1},... | collective-permute-start | bytes 589832 | tf_op jit(solution)/shard_map/ppermute | solution.py:21
  96.8 9.7 %collective-permute-start.27 = (bf16[96,1024]{1,0:T(8,128)(2,1)S(1)}, bf16[96,1024]{1,0:T(8,128)(2,1)S(1)}, u32[]{:S(2)}, u32[]{:S(2)}) collective-permute-start(bf16[96,1024]{1,0:T(8,128)(2,1)S(1)} %shard_map.69.refs_0_), channel_id=1, source_target_pairs={{0,4},{1,5},{2,6},{3,7},{4,0},{5,1},{6,2},{7,3},{8,12},{9,13},{10,... | collective-permute-start | bytes 589832 | tf_op jit(solution)/shard_map/ppermute | solution.py:21
  96.9 12.1 %collective-permute-start.25 = (bf16[96,1024]{1,0:T(8,128)(2,1)S(1)}, bf16[96,1024]{1,0:T(8,128)(2,1)S(1)}, u32[]{:S(2)}, u32[]{:S(2)}) collective-permute-start(bf16[96,1024]{1,0:T(8,128)(2,1)S(1)} %shard_map.69.refs_0_), channel_id=1, source_target_pairs={{0,12},{1,13},{2,14},{3,15},{4,8},{5,9},{6,10},{7,11},{8,4},{9,5},... | collective-permute-start | bytes 589832 | tf_op jit(solution)/shard_map/ppermute | solution.py:21
  99.0 16.8 %collective-permute-start.23 = (bf16[96,1024]{1,0:T(8,128)(2,1)S(1)}, bf16[96,1024]{1,0:T(8,128)(2,1)S(1)}, u32[]{:S(2)}, u32[]{:S(2)}) collective-permute-start(bf16[96,1024]{1,0:T(8,128)(2,1)S(1)} %shard_map.69.refs_0_), channel_id=1, source_target_pairs={{0,8},{1,9},{2,10},{3,11},{4,12},{5,13},{6,14},{7,15},{8,0},{9,1},... | collective-permute-start | bytes 589832 | tf_op jit(solution)/shard_map/ppermute | solution.py:21
  100.4 16.5 %collective-permute-start.28 = (bf16[96,1024]{1,0:T(8,128)(2,1)S(1)}, bf16[96,1024]{1,0:T(8,128)(2,1)S(1)}, u32[]{:S(2)}, u32[]{:S(2)}) collective-permute-start(bf16[96,1024]{1,0:T(8,128)(2,1)S(1)} %shard_map.69.refs_0_), channel_id=1, source_target_pairs={{0,2},{1,3},{2,0},{3,1},{4,6},{5,7},{6,4},{7,5},{8,10},{9,11},{10,... | collective-permute-start | bytes 589832 | tf_op jit(solution)/shard_map/ppermute | solution.py:21
  106.5 10.3 %collective-permute-start.29 = (bf16[96,1024]{1,0:T(8,128)(2,1)S(1)}, bf16[96,1024]{1,0:T(8,128)(2,1)S(1)}, u32[]{:S(2)}, u32[]{:S(2)}) collective-permute-start(bf16[96,1024]{1,0:T(8,128)(2,1)S(1)} %collective-permute-done.27.refs_1_), channel_id=1, source_target_pairs={{0,2},{1,3},{2,0},{3,1},{4,6},{5,7},{6,4},{7,5},{8,10},{9,11},{10,... | collective-permute-start | bytes 589832 | tf_op jit(solution)/shard_map/ppermute | solution.py:21
  109.0 9.8 %collective-permute-start.26 = (bf16[96,1024]{1,0:T(8,128)(2,1)S(1)}, bf16[96,1024]{1,0:T(8,128)(2,1)S(1)}, u32[]{:S(2)}, u32[]{:S(2)}) collective-permute-start(bf16[96,1024]{1,0:T(8,128)(2,1)S(1)} %collective-permute-done.25.refs_2_), channel_id=1, source_target_pairs={{0,2},{1,3},{2,0},{3,1},{4,6},{5,7},{6,4},{7,5},{8,10},{9,11},{10,... | collective-permute-start | bytes 589832 | tf_op jit(solution)/shard_map/ppermute | solution.py:21
  136.7 10.9 %collective-permute-start.38 = (bf16[96,1024]{1,0:T(8,128)(2,1)S(1)}, bf16[96,1024]{1,0:T(8,128)(2,1)S(1)}, u32[]{:S(2)}, u32[]{:S(2)}) collective-permute-start(bf16[96,1024]{1,0:T(8,128)(2,1)S(1)} %get-tuple-element.45), channel_id=1, source_target_pairs={{0,2},{1,3},{2,0},{3,1},{4,6},{5,7},{6,4},{7,5},{8,10},{9,11},{10,... | collective-permute-start | bytes 589832 | tf_op jit(solution)/shard_map/ppermute | solution.py:21
  137.6 14.0 %collective-permute-start.36 = (bf16[96,1024]{1,0:T(8,128)(2,1)S(1)}, bf16[96,1024]{1,0:T(8,128)(2,1)S(1)}, u32[]{:S(2)}, u32[]{:S(2)}) collective-permute-start(bf16[96,1024]{1,0:T(8,128)(2,1)S(1)} %shard_map.77), channel_id=1, source_target_pairs={{0,2},{1,3},{2,0},{3,1},{4,6},{5,7},{6,4},{7,5},{8,10},{9,11},{10,... | collective-permute-start | bytes 589832 | tf_op jit(solution)/shard_map/ppermute | solution.py:21
  138.7 15.0 %collective-permute-start.35 = (bf16[96,1024]{1,0:T(8,128)(2,1)S(1)}, bf16[96,1024]{1,0:T(8,128)(2,1)S(1)}, u32[]{:S(2)}, u32[]{:S(2)}) collective-permute-start(bf16[96,1024]{1,0:T(8,128)(2,1)S(1)} %get-tuple-element.42), channel_id=1, source_target_pairs={{0,2},{1,3},{2,0},{3,1},{4,6},{5,7},{6,4},{7,5},{8,10},{9,11},{10,... | collective-permute-start | bytes 589832 | tf_op jit(solution)/shard_map/ppermute | solution.py:21
  143.6 10.1 %collective-permute-start.41 = (bf16[96,1024]{1,0:T(8,128)(2,1)S(1)}, bf16[96,1024]{1,0:T(8,128)(2,1)S(1)}, u32[]{:S(2)}, u32[]{:S(2)}) collective-permute-start(bf16[96,1024]{1,0:T(8,128)(2,1)S(1)} %add_convert_fusion), channel_id=1, source_target_pairs={{0,4},{1,5},{2,6},{3,7},{4,0},{5,1},{6,2},{7,3},{8,12},{9,13},{10,... | collective-permute-start | bytes 589832 | tf_op jit(solution)/shard_map/ppermute | solution.py:21
  151.6 12.2 %collective-permute-start.37 = (bf16[96,1024]{1,0:T(8,128)(2,1)S(1)}, bf16[96,1024]{1,0:T(8,128)(2,1)S(1)}, u32[]{:S(2)}, u32[]{:S(2)}) collective-permute-start(bf16[96,1024]{1,0:T(8,128)(2,1)S(1)} %add_convert_fusion.2), channel_id=1, source_target_pairs={{0,8},{1,9},{2,10},{3,11},{4,12},{5,13},{6,14},{7,15},{8,0},{9,1},... | collective-permute-start | bytes 589832 | tf_op jit(solution)/shard_map/ppermute | solution.py:21
  (23 other events, 168.4 us)

commit v3 on v2

--- a/solution.py
+++ b/solution.py
@@ -63,7 +63,7 @@
             out_ref[at, i * strike:(i + 1) * strike] = rows[width + i].astype(bf16)
         return 0
 
-    lax.fori_loop(0, columns // 8, group, 0, unroll=2)
+    lax.fori_loop(0, columns // 8, group, 0, unroll=4)
 
 
 def smooth(sketch):
@@ -285,7 +285,7 @@
     n = lax.axis_size("row")
     if not direct(n):
         return lax.psum(x, "row", axis_index_groups=same_core())
-    far = [swap(x, 4 * k) for k in range(1, n // 4)]
+    far = [swap(x, 2 * k) for k in order(n // 2)[::-1] if k]
     x = sum(far, x)
     return x + swap(x, 2)
 
@@ -342,9 +342,13 @@
 
         sent = call([ks[0] + 1], bf16) + call([k + 1 for k in ks[1:]], bf16)
         kept = call(ks, f32)
-        sums = [a + swap(v, 2).astype(f32) for a, v in zip(kept, sent)]
-        far = [swap(v.astype(bf16), 2 * k) for v, k in zip(sums, ks) if k]
-        return [sums[-1]] + far
+        far = []
+        for a, v, k in zip(kept, sent, ks):
+            got = swap(v, 2)
+            if k == 0:
+                return [a + got.astype(f32)] + far
+            v = (a + got.astype(f32)).astype(bf16)
+            far.append(swap(v, 2 * k))
 
     _, weighted, gram = finish(*forward(omega, True), weights, float(params))
     pieces = backward(weighted)

time: 165 us -> 165 us (level)
  waiting for transfers between devices: 80.5 us -> 77 us
  starting transfers between devices: 44.2 us -> 47.6 us
    ppermute x40, waiting for transfers between devices: 76.5 us -> 72.9 us  [swap(): return lax.ppermute(x, 'row', [(i, i ^ k) for i in range(n)])]
    ppermute x40, starting transfers between devices: 41 us -> 44.3 us  [swap(): return lax.ppermute(x, 'row', [(i, i ^ k) for i in range(n)])]
where the time goes in v3:
time: 165 us; the launch traced here: 164 us
  waiting for transfers between devices  77 us (47%)
  starting transfers between devices  47.6 us (29%)
  Pallas kernels  34.1 us (21%)
  local copies, waits for them, and re-layouts  3.2 us (2%)
    ppermute x40, waiting for transfers between devices, swap(): return lax.ppermute(x, 'row', [(i, i ^ k) for i in range(n)])  72.9 us
    ppermute x40, starting transfers between devices, swap(): return lax.ppermute(x, 'row', [(i, i ^ k) for i in range(n)])  44.3 us
    pallas_call x18, Pallas kernels, small_call(): pl.pallas_call(kernel, out_shape=outs, in_specs=[pl.BlockSpec(memory_spac...  22.3 us
    pallas_call x2, Pallas kernels, pick(): pl.pallas_call(pick_kernel, out_shape=out((chips, greens.shape[0], block)...  6.49 us
    ppermute x1, waiting for transfers between devices, halo_rows(): before.insert(0, lax.ppermute(x[:, length - take:], 'row', up))  3.87 us
  transfers between devices with their start and end apart: 42, of which 26 were waited for; matrix products, arithmetic and copies ran while one was open for 1% of the time, Pallas kernels for 14%

profile of v3, /device:TPU:0, one launch (start us, length us, event | category | flops | bytes accessed | tf_op | source)
XLA Modules:
  0.0 164.3 jit_solution(4374178788993508775)
XLA Ops:
  0.7 4.3 %shard_map.60 = bf16[8,256,1024]{2,1,0:T(8,128)(2,1)} custom-call(s32[1]{0:T(128)} %bitcast.2.core_ref, bf16[256,16384]{1,0:T(8,128)(2,1)} %in_ref.3), custom_call_target="tpu_custom_call" | custom-call | tf_op jit(solution)/shard_map/pallas_call | solution.py:163
  8.9 3.9 %collective-permute-done.1.before_ref = f32[96,4,128]{2,1,0:T(4,128)S(1)} collective-permute-done((f32[96,4,128]{2,1,0:T(4,128)S(1)}, f32[96,4,128]{2,1,0:T(4,128)S(1)}, u32[]{:S(2)}, u32[]{:S(2)}) %collective-permute-start.1) | collective-permute-done | bytes 196640 | tf_op jit(solution)/shard_map/ppermute | solution.py:32
  13.0 2.9 %smooth.1.refs_0_ = bf16[96,1024]{1,0:T(8,128)(2,1)S(1)} custom-call(s32[2]{0:T(128)S(1)} %pad_add_fusion.edge_ref, f32[96,4,128]{2,1,0:T(4,128)S(1)} %collective-permute-done.1.before_ref, f32[96,8,128]{2,1,0:T(8,128)S(1)} %copy-done.3, f32[96,4,128]{2,1,0:T(4,128)S(1)} %collective-permute-done.2.after_ref), custom_call_target="tpu_custom_call" | custom-call | tf_op jit(solution)/shard_map/smooth/pallas_call | solution.py:75
  15.9 4.9 %collective-permute-start.7 = (bf16[96,1024]{1,0:T(8,128)(2,1)S(1)}, bf16[96,1024]{1,0:T(8,128)(2,1)S(1)}, u32[]{:S(2)}, u32[]{:S(2)}) collective-permute-start(bf16[96,1024]{1,0:T(8,128)(2,1)S(1)} %smooth.1.refs_0_), channel_id=1, source_target_pairs={{0,4},{1,5},{2,6},{3,7},{4,0},{5,1},{6,2},{7,3},{8,12},{9,13},{10,... | collective-permute-start | bytes 589832 | tf_op jit(solution)/shard_map/ppermute | solution.py:21
  20.8 2.5 %collective-permute-start.5 = (bf16[96,1024]{1,0:T(8,128)(2,1)S(1)}, bf16[96,1024]{1,0:T(8,128)(2,1)S(1)}, u32[]{:S(2)}, u32[]{:S(2)}) collective-permute-start(bf16[96,1024]{1,0:T(8,128)(2,1)S(1)} %smooth.1.refs_0_), channel_id=1, source_target_pairs={{0,12},{1,13},{2,14},{3,15},{4,8},{5,9},{6,10},{7,11},{8,4},{9,5},... | collective-permute-start | bytes 589832 | tf_op jit(solution)/shard_map/ppermute | solution.py:21
  24.0 2.2 %collective-permute-done.7.refs_1_ = bf16[96,1024]{1,0:T(8,128)(2,1)S(1)} collective-permute-done((bf16[96,1024]{1,0:T(8,128)(2,1)S(1)}, bf16[96,1024]{1,0:T(8,128)(2,1)S(1)}, u32[]{:S(2)}, u32[]{:S(2)}) %collective-permute-start.7) | collective-permute-done | bytes 196640 | tf_op jit(solution)/shard_map/ppermute | solution.py:21
  26.2 7.2 %collective-permute-done.5.refs_2_ = bf16[96,1024]{1,0:T(8,128)(2,1)S(1)} collective-permute-done((bf16[96,1024]{1,0:T(8,128)(2,1)S(1)}, bf16[96,1024]{1,0:T(8,128)(2,1)S(1)}, u32[]{:S(2)}, u32[]{:S(2)}) %collective-permute-start.5) | collective-permute-done | bytes 196640 | tf_op jit(solution)/shard_map/ppermute | solution.py:21
  33.3 8.4 %collective-permute-done.3.refs_0_ = bf16[96,1024]{1,0:T(8,128)(2,1)S(1)} collective-permute-done((bf16[96,1024]{1,0:T(8,128)(2,1)S(1)}, bf16[96,1024]{1,0:T(8,128)(2,1)S(1)}, u32[]{:S(2)}, u32[]{:S(2)}) %collective-permute-start.3) | collective-permute-done | bytes 196640 | tf_op jit(solution)/shard_map/ppermute | solution.py:21
  41.7 2.2 %shard_map.59.mine_ref = bf16[8,256,1024]{2,1,0:T(8,128)(2,1)S(1)} custom-call(s32[1]{0:T(128)} %bitcast.1.core_ref, bf16[256,16384]{1,0:T(8,128)(2,1)} %in_ref.3), custom_call_target="tpu_custom_call" | custom-call | tf_op jit(solution)/shard_map/pallas_call | solution.py:163
  46.0 2.4 %keep_theirs.1.theirs_ref = bf16[8,256,1024]{2,1,0:T(8,128)(2,1)S(1)} custom-call(bf16[8,256,1024]{2,1,0:T(8,128)(2,1)} %collective-permute-done.in_ref), custom_call_target="tpu_custom_call" | custom-call | tf_op jit(solution)/shard_map/keep_theirs/pallas_call | solution.py:178
  54.6 4.2 %shard_map.64 = (f32[96,512]{1,0:T(8,128)}, bf16[96,512]{1,0:T(8,128)(2,1)S(1)}, f32[96,96]{1,0:T(8,128)S(1)}) custom-call(f32[96,640]{1,0:T(8,128)S(1)} %get-tuple-element.25.total_ref, f32[96,640]{1,0:T(8,128)S(1)} %collective-permute-done.10.other_ref, f32[1,512]{1,0:T(1,128)S(1)} %bitcast.12), custom_call_target="tpu_custom_call" | custom-call | tf_op jit(solution)/shard_map/pallas_call | solution.py:133
  58.8 3.3 %collective-permute-start.13 = (f32[96,96]{1,0:T(8,128)S(1)}, f32[96,96]{1,0:T(8,128)S(1)}, u32[]{:S(2)}, u32[]{:S(2)}) collective-permute-start(f32[96,96]{1,0:T(8,128)S(1)} %get-tuple-element.27), channel_id=1, source_target_pairs={{0,12},{1,13},{2,14},{3,15},{4,8},{5,9},{6,10},{7,11},{8,4},{9,5},... | collective-permute-start | bytes 110600 | tf_op jit(solution)/shard_map/ppermute | solution.py:21
  72.2 3.0 %shard_map.65.inv_ref = f32[96,96]{1,0:T(8,128)S(1)} custom-call(f32[96,96]{1,0:T(8,128)S(1)} %add.57.gram_ref), custom_call_target="tpu_custom_call" | custom-call | tf_op jit(solution)/shard_map/pallas_call | solution.py:133
  79.5 2.5 %collective-permute-done.17 = bf16[96,1024]{1,0:T(8,128)(2,1)S(1)} collective-permute-done((bf16[96,1024]{1,0:T(8,128)(2,1)S(1)}, bf16[96,1024]{1,0:T(8,128)(2,1)S(1)}, u32[]{:S(2)}, u32[]{:S(2)}) %collective-permute-start.17) | collective-permute-done | bytes 196640 | tf_op jit(solution)/shard_map/ppermute | solution.py:21
  85.1 2.9 %collective-permute-done.20.refs_1_ = bf16[96,1024]{1,0:T(8,128)(2,1)S(1)} collective-permute-done((bf16[96,1024]{1,0:T(8,128)(2,1)S(1)}, bf16[96,1024]{1,0:T(8,128)(2,1)S(1)}, u32[]{:S(2)}, u32[]{:S(2)}) %collective-permute-start.20) | collective-permute-done | bytes 196640 | tf_op jit(solution)/shard_map/ppermute | solution.py:21
  87.9 7.5 %collective-permute-done.18.refs_0_ = bf16[96,1024]{1,0:T(8,128)(2,1)S(1)} collective-permute-done((bf16[96,1024]{1,0:T(8,128)(2,1)S(1)}, bf16[96,1024]{1,0:T(8,128)(2,1)S(1)}, u32[]{:S(2)}, u32[]{:S(2)}) %collective-permute-start.18) | collective-permute-done | bytes 196640 | tf_op jit(solution)/shard_map/ppermute | solution.py:21
  101.0 3.4 %collective-permute-done.27.refs_1_ = bf16[96,1024]{1,0:T(8,128)(2,1)S(1)} collective-permute-done((bf16[96,1024]{1,0:T(8,128)(2,1)S(1)}, bf16[96,1024]{1,0:T(8,128)(2,1)S(1)}, u32[]{:S(2)}, u32[]{:S(2)}) %collective-permute-start.27) | collective-permute-done | bytes 196640 | tf_op jit(solution)/shard_map/ppermute | solution.py:21
  104.4 2.7 %collective-permute-start.29 = (bf16[96,1024]{1,0:T(8,128)(2,1)S(1)}, bf16[96,1024]{1,0:T(8,128)(2,1)S(1)}, u32[]{:S(2)}, u32[]{:S(2)}) collective-permute-start(bf16[96,1024]{1,0:T(8,128)(2,1)S(1)} %collective-permute-done.27.refs_1_), channel_id=1, source_target_pairs={{0,2},{1,3},{2,0},{3,1},{4,6},{5,7},{6,4},{7,5},{8,10},{9,11},{10,... | collective-permute-start | bytes 589832 | tf_op jit(solution)/shard_map/ppermute | solution.py:21
  109.0 6.6 %collective-permute-done.23.refs_0_ = bf16[96,1024]{1,0:T(8,128)(2,1)S(1)} collective-permute-done((bf16[96,1024]{1,0:T(8,128)(2,1)S(1)}, bf16[96,1024]{1,0:T(8,128)(2,1)S(1)}, u32[]{:S(2)}, u32[]{:S(2)}) %collective-permute-start.23) | collective-permute-done | bytes 196640 | tf_op jit(solution)/shard_map/ppermute | solution.py:21
  127.1 2.8 %collective-permute-done.31 = f32[96,96]{1,0:T(8,128)S(1)} collective-permute-done((f32[96,96]{1,0:T(8,128)S(1)}, f32[96,96]{1,0:T(8,128)S(1)}, u32[]{:S(2)}, u32[]{:S(2)}) %collective-permute-start.31) | collective-permute-done | bytes 36896 | tf_op jit(solution)/shard_map/ppermute | solution.py:21
  138.4 3.0 %shard_map.74.inv_ref = f32[96,96]{1,0:T(8,128)S(1)} custom-call(f32[96,96]{1,0:T(8,128)S(1)} %add.65.gram_ref), custom_call_target="tpu_custom_call" | custom-call | tf_op jit(solution)/shard_map/pallas_call | solution.py:133
  143.1 3.2 %collective-permute-done.38 = bf16[96,1024]{1,0:T(8,128)(2,1)S(1)} collective-permute-done((bf16[96,1024]{1,0:T(8,128)(2,1)S(1)}, bf16[96,1024]{1,0:T(8,128)(2,1)S(1)}, u32[]{:S(2)}, u32[]{:S(2)}) %collective-permute-start.38) | collective-permute-done | bytes 196640 | tf_op jit(solution)/shard_map/ppermute | solution.py:21
  148.1 2.4 %collective-permute-done.36 = bf16[96,1024]{1,0:T(8,128)(2,1)S(1)} collective-permute-done((bf16[96,1024]{1,0:T(8,128)(2,1)S(1)}, bf16[96,1024]{1,0:T(8,128)(2,1)S(1)}, u32[]{:S(2)}, u32[]{:S(2)}) %collective-permute-start.36) | collective-permute-done | bytes 196640 | tf_op jit(solution)/shard_map/ppermute | solution.py:21
  155.3 7.7 %collective-permute-done.37.refs_0_ = bf16[96,1024]{1,0:T(8,128)(2,1)S(1)} collective-permute-done((bf16[96,1024]{1,0:T(8,128)(2,1)S(1)}, bf16[96,1024]{1,0:T(8,128)(2,1)S(1)}, u32[]{:S(2)}, u32[]{:S(2)}) %collective-permute-start.37) | collective-permute-done | bytes 196640 | tf_op jit(solution)/shard_map/ppermute | solution.py:21
  (109 shorter events, 67.2 us)
Async XLA Ops:
  4.9 41.1 %collective-permute-start = (bf16[8,256,1024]{2,1,0:T(8,128)(2,1)}, bf16[8,256,1024]{2,1,0:T(8,128)(2,1)}, u32[]{:S(2)}, u32[]{:S(2)}) collective-permute-start(bf16[8,256,1024]{2,1,0:T(8,128)(2,1)} %shard_map.60), channel_id=1, source_target_pairs={{0,1},{1,0},{2,3},{3,2},{4,5},{5,4},{6,7},{7,6},{8,9},{9,8},{10,11... | collective-permute-start | bytes 12582920 | tf_op jit(solution)/shard_map/ppermute | solution.py:21
  15.9 10.3 %collective-permute-start.7 = (bf16[96,1024]{1,0:T(8,128)(2,1)S(1)}, bf16[96,1024]{1,0:T(8,128)(2,1)S(1)}, u32[]{:S(2)}, u32[]{:S(2)}) collective-permute-start(bf16[96,1024]{1,0:T(8,128)(2,1)S(1)} %smooth.1.refs_0_), channel_id=1, source_target_pairs={{0,4},{1,5},{2,6},{3,7},{4,0},{5,1},{6,2},{7,3},{8,12},{9,13},{10,... | collective-permute-start | bytes 589832 | tf_op jit(solution)/shard_map/ppermute | solution.py:21
  20.8 12.5 %collective-permute-start.5 = (bf16[96,1024]{1,0:T(8,128)(2,1)S(1)}, bf16[96,1024]{1,0:T(8,128)(2,1)S(1)}, u32[]{:S(2)}, u32[]{:S(2)}) collective-permute-start(bf16[96,1024]{1,0:T(8,128)(2,1)S(1)} %smooth.1.refs_0_), channel_id=1, source_target_pairs={{0,12},{1,13},{2,14},{3,15},{4,8},{5,9},{6,10},{7,11},{8,4},{9,5},... | collective-permute-start | bytes 589832 | tf_op jit(solution)/shard_map/ppermute | solution.py:21
  23.3 18.4 %collective-permute-start.3 = (bf16[96,1024]{1,0:T(8,128)(2,1)S(1)}, bf16[96,1024]{1,0:T(8,128)(2,1)S(1)}, u32[]{:S(2)}, u32[]{:S(2)}) collective-permute-start(bf16[96,1024]{1,0:T(8,128)(2,1)S(1)} %smooth.1.refs_0_), channel_id=1, source_target_pairs={{0,8},{1,9},{2,10},{3,11},{4,12},{5,13},{6,14},{7,15},{8,0},{9,1},... | collective-permute-start | bytes 589832 | tf_op jit(solution)/shard_map/ppermute | solution.py:21
  23.4 25.0 %collective-permute-start.8 = (bf16[96,1024]{1,0:T(8,128)(2,1)S(1)}, bf16[96,1024]{1,0:T(8,128)(2,1)S(1)}, u32[]{:S(2)}, u32[]{:S(2)}) collective-permute-start(bf16[96,1024]{1,0:T(8,128)(2,1)S(1)} %smooth.1.refs_0_), channel_id=1, source_target_pairs={{0,2},{1,3},{2,0},{3,1},{4,6},{5,7},{6,4},{7,5},{8,10},{9,11},{10,... | collective-permute-start | bytes 589832 | tf_op jit(solution)/shard_map/ppermute | solution.py:21
  26.2 22.2 %collective-permute-start.9 = (bf16[96,1024]{1,0:T(8,128)(2,1)S(1)}, bf16[96,1024]{1,0:T(8,128)(2,1)S(1)}, u32[]{:S(2)}, u32[]{:S(2)}) collective-permute-start(bf16[96,1024]{1,0:T(8,128)(2,1)S(1)} %collective-permute-done.7.refs_1_), channel_id=1, source_target_pairs={{0,2},{1,3},{2,0},{3,1},{4,6},{5,7},{6,4},{7,5},{8,10},{9,11},{10,... | collective-permute-start | bytes 589832 | tf_op jit(solution)/shard_map/ppermute | solution.py:21
  33.3 18.1 %collective-permute-start.6 = (bf16[96,1024]{1,0:T(8,128)(2,1)S(1)}, bf16[96,1024]{1,0:T(8,128)(2,1)S(1)}, u32[]{:S(2)}, u32[]{:S(2)}) collective-permute-start(bf16[96,1024]{1,0:T(8,128)(2,1)S(1)} %collective-permute-done.5.refs_2_), channel_id=1, source_target_pairs={{0,2},{1,3},{2,0},{3,1},{4,6},{5,7},{6,4},{7,5},{8,10},{9,11},{10,... | collective-permute-start | bytes 589832 | tf_op jit(solution)/shard_map/ppermute | solution.py:21
  41.7 10.6 %collective-permute-start.4 = (bf16[96,1024]{1,0:T(8,128)(2,1)S(1)}, bf16[96,1024]{1,0:T(8,128)(2,1)S(1)}, u32[]{:S(2)}, u32[]{:S(2)}) collective-permute-start(bf16[96,1024]{1,0:T(8,128)(2,1)S(1)} %collective-permute-done.3.refs_0_), channel_id=1, source_target_pairs={{0,2},{1,3},{2,0},{3,1},{4,6},{5,7},{6,4},{7,5},{8,10},{9,11},{10,... | collective-permute-start | bytes 589832 | tf_op jit(solution)/shard_map/ppermute | solution.py:21
  63.3 12.0 %collective-permute-start.21 = (bf16[96,1024]{1,0:T(8,128)(2,1)S(1)}, bf16[96,1024]{1,0:T(8,128)(2,1)S(1)}, u32[]{:S(2)}, u32[]{:S(2)}) collective-permute-start(bf16[96,1024]{1,0:T(8,128)(2,1)S(1)} %get-tuple-element.35), channel_id=1, source_target_pairs={{0,2},{1,3},{2,0},{3,1},{4,6},{5,7},{6,4},{7,5},{8,10},{9,11},{10,... | collective-permute-start | bytes 589832 | tf_op jit(solution)/shard_map/ppermute | solution.py:21
  70.2 11.8 %collective-permute-start.17 = (bf16[96,1024]{1,0:T(8,128)(2,1)S(1)}, bf16[96,1024]{1,0:T(8,128)(2,1)S(1)}, u32[]{:S(2)}, u32[]{:S(2)}) collective-permute-start(bf16[96,1024]{1,0:T(8,128)(2,1)S(1)} %shard_map.68), channel_id=1, source_target_pairs={{0,2},{1,3},{2,0},{3,1},{4,6},{5,7},{6,4},{7,5},{8,10},{9,11},{10,... | collective-permute-start | bytes 589832 | tf_op jit(solution)/shard_map/ppermute | solution.py:21
  72.1 12.9 %collective-permute-start.16 = (bf16[96,1024]{1,0:T(8,128)(2,1)S(1)}, bf16[96,1024]{1,0:T(8,128)(2,1)S(1)}, u32[]{:S(2)}, u32[]{:S(2)}) collective-permute-start(bf16[96,1024]{1,0:T(8,128)(2,1)S(1)} %get-tuple-element.30), channel_id=1, source_target_pairs={{0,2},{1,3},{2,0},{3,1},{4,6},{5,7},{6,4},{7,5},{8,10},{9,11},{10,... | collective-permute-start | bytes 589832 | tf_op jit(solution)/shard_map/ppermute | solution.py:21
  75.3 9.7 %collective-permute-start.22 = (bf16[96,1024]{1,0:T(8,128)(2,1)S(1)}, bf16[96,1024]{1,0:T(8,128)(2,1)S(1)}, u32[]{:S(2)}, u32[]{:S(2)}) collective-permute-start(bf16[96,1024]{1,0:T(8,128)(2,1)S(1)} %add_convert_fusion.3), channel_id=1, source_target_pairs={{0,4},{1,5},{2,6},{3,7},{4,0},{5,1},{6,2},{7,3},{8,12},{9,13},{10,... | collective-permute-start | bytes 589832 | tf_op jit(solution)/shard_map/ppermute | solution.py:21
  77.9 10.1 %collective-permute-start.20 = (bf16[96,1024]{1,0:T(8,128)(2,1)S(1)}, bf16[96,1024]{1,0:T(8,128)(2,1)S(1)}, u32[]{:S(2)}, u32[]{:S(2)}) collective-permute-start(bf16[96,1024]{1,0:T(8,128)(2,1)S(1)} %add_convert_fusion.4), channel_id=1, source_target_pairs={{0,12},{1,13},{2,14},{3,15},{4,8},{5,9},{6,10},{7,11},{8,4},{9,5},... | collective-permute-start | bytes 589832 | tf_op jit(solution)/shard_map/ppermute | solution.py:21
  82.1 13.4 %collective-permute-start.18 = (bf16[96,1024]{1,0:T(8,128)(2,1)S(1)}, bf16[96,1024]{1,0:T(8,128)(2,1)S(1)}, u32[]{:S(2)}, u32[]{:S(2)}) collective-permute-start(bf16[96,1024]{1,0:T(8,128)(2,1)S(1)} %add_convert_fusion.5), channel_id=1, source_target_pairs={{0,8},{1,9},{2,10},{3,11},{4,12},{5,13},{6,14},{7,15},{8,0},{9,1},... | collective-permute-start | bytes 589832 | tf_op jit(solution)/shard_map/ppermute | solution.py:21
  96.1 11.8 %collective-permute-start.25 = (bf16[96,1024]{1,0:T(8,128)(2,1)S(1)}, bf16[96,1024]{1,0:T(8,128)(2,1)S(1)}, u32[]{:S(2)}, u32[]{:S(2)}) collective-permute-start(bf16[96,1024]{1,0:T(8,128)(2,1)S(1)} %shard_map.69.refs_0_), channel_id=1, source_target_pairs={{0,12},{1,13},{2,14},{3,15},{4,8},{5,9},{6,10},{7,11},{8,4},{9,5},... | collective-permute-start | bytes 589832 | tf_op jit(solution)/shard_map/ppermute | solution.py:21
  97.9 17.7 %collective-permute-start.23 = (bf16[96,1024]{1,0:T(8,128)(2,1)S(1)}, bf16[96,1024]{1,0:T(8,128)(2,1)S(1)}, u32[]{:S(2)}, u32[]{:S(2)}) collective-permute-start(bf16[96,1024]{1,0:T(8,128)(2,1)S(1)} %shard_map.69.refs_0_), channel_id=1, source_target_pairs={{0,8},{1,9},{2,10},{3,11},{4,12},{5,13},{6,14},{7,15},{8,0},{9,1},... | collective-permute-start | bytes 589832 | tf_op jit(solution)/shard_map/ppermute | solution.py:21
  99.6 17.0 %collective-permute-start.28 = (bf16[96,1024]{1,0:T(8,128)(2,1)S(1)}, bf16[96,1024]{1,0:T(8,128)(2,1)S(1)}, u32[]{:S(2)}, u32[]{:S(2)}) collective-permute-start(bf16[96,1024]{1,0:T(8,128)(2,1)S(1)} %shard_map.69.refs_0_), channel_id=1, source_target_pairs={{0,2},{1,3},{2,0},{3,1},{4,6},{5,7},{6,4},{7,5},{8,10},{9,11},{10,... | collective-permute-start | bytes 589832 | tf_op jit(solution)/shard_map/ppermute | solution.py:21
  104.4 12.2 %collective-permute-start.29 = (bf16[96,1024]{1,0:T(8,128)(2,1)S(1)}, bf16[96,1024]{1,0:T(8,128)(2,1)S(1)}, u32[]{:S(2)}, u32[]{:S(2)}) collective-permute-start(bf16[96,1024]{1,0:T(8,128)(2,1)S(1)} %collective-permute-done.27.refs_1_), channel_id=1, source_target_pairs={{0,2},{1,3},{2,0},{3,1},{4,6},{5,7},{6,4},{7,5},{8,10},{9,11},{10,... | collective-permute-start | bytes 589832 | tf_op jit(solution)/shard_map/ppermute | solution.py:21
  107.9 10.7 %collective-permute-start.26 = (bf16[96,1024]{1,0:T(8,128)(2,1)S(1)}, bf16[96,1024]{1,0:T(8,128)(2,1)S(1)}, u32[]{:S(2)}, u32[]{:S(2)}) collective-permute-start(bf16[96,1024]{1,0:T(8,128)(2,1)S(1)} %collective-permute-done.25.refs_2_), channel_id=1, source_target_pairs={{0,2},{1,3},{2,0},{3,1},{4,6},{5,7},{6,4},{7,5},{8,10},{9,11},{10,... | collective-permute-start | bytes 589832 | tf_op jit(solution)/shard_map/ppermute | solution.py:21
  135.2 11.1 %collective-permute-start.38 = (bf16[96,1024]{1,0:T(8,128)(2,1)S(1)}, bf16[96,1024]{1,0:T(8,128)(2,1)S(1)}, u32[]{:S(2)}, u32[]{:S(2)}) collective-permute-start(bf16[96,1024]{1,0:T(8,128)(2,1)S(1)} %get-tuple-element.45), channel_id=1, source_target_pairs={{0,2},{1,3},{2,0},{3,1},{4,6},{5,7},{6,4},{7,5},{8,10},{9,11},{10,... | collective-permute-start | bytes 589832 | tf_op jit(solution)/shard_map/ppermute | solution.py:21
  136.3 14.2 %collective-permute-start.36 = (bf16[96,1024]{1,0:T(8,128)(2,1)S(1)}, bf16[96,1024]{1,0:T(8,128)(2,1)S(1)}, u32[]{:S(2)}, u32[]{:S(2)}) collective-permute-start(bf16[96,1024]{1,0:T(8,128)(2,1)S(1)} %shard_map.77), channel_id=1, source_target_pairs={{0,2},{1,3},{2,0},{3,1},{4,6},{5,7},{6,4},{7,5},{8,10},{9,11},{10,... | collective-permute-start | bytes 589832 | tf_op jit(solution)/shard_map/ppermute | solution.py:21
  137.2 15.9 %collective-permute-start.35 = (bf16[96,1024]{1,0:T(8,128)(2,1)S(1)}, bf16[96,1024]{1,0:T(8,128)(2,1)S(1)}, u32[]{:S(2)}, u32[]{:S(2)}) collective-permute-start(bf16[96,1024]{1,0:T(8,128)(2,1)S(1)} %get-tuple-element.42), channel_id=1, source_target_pairs={{0,2},{1,3},{2,0},{3,1},{4,6},{5,7},{6,4},{7,5},{8,10},{9,11},{10,... | collective-permute-start | bytes 589832 | tf_op jit(solution)/shard_map/ppermute | solution.py:21
  142.4 10.8 %collective-permute-start.41 = (bf16[96,1024]{1,0:T(8,128)(2,1)S(1)}, bf16[96,1024]{1,0:T(8,128)(2,1)S(1)}, u32[]{:S(2)}, u32[]{:S(2)}) collective-permute-start(bf16[96,1024]{1,0:T(8,128)(2,1)S(1)} %add_convert_fusion), channel_id=1, source_target_pairs={{0,4},{1,5},{2,6},{3,7},{4,0},{5,1},{6,2},{7,3},{8,12},{9,13},{10,... | collective-permute-start | bytes 589832 | tf_op jit(solution)/shard_map/ppermute | solution.py:21
  150.6 12.5 %collective-permute-start.37 = (bf16[96,1024]{1,0:T(8,128)(2,1)S(1)}, bf16[96,1024]{1,0:T(8,128)(2,1)S(1)}, u32[]{:S(2)}, u32[]{:S(2)}) collective-permute-start(bf16[96,1024]{1,0:T(8,128)(2,1)S(1)} %add_convert_fusion.2), channel_id=1, source_target_pairs={{0,8},{1,9},{2,10},{3,11},{4,12},{5,13},{6,14},{7,15},{8,0},{9,1},... | collective-permute-start | bytes 589832 | tf_op jit(solution)/shard_map/ppermute | solution.py:21
  (23 other events, 169.2 us)
